TPU v7x, 256 devices: a whole 4x4x8 slice. The times are simulated.
256 devices in a mesh: tower: 4 (over y), dp: 64 (over z, x, core).
Axes of the slice: x: 4, y: 4, z: 8, core: 2. Of those that a mesh axis runs over, the one named last changes fastest.
Arguments:
- query_hidden: bfloat16 [12288, 2304], P('dp'), may hold values from -6 to 6
- passage_hidden: bfloat16 [12288, 3072], P(('tower', 'dp')), may hold values from -6 to 6
- pool_hidden: bfloat16 [131072, 3072], P(('tower', 'dp')), may hold values from -6 to 6
- query_proj: bfloat16 [2304, 768], replicated, may hold values from -0.125 to 0.125
- passage_proj: bfloat16 [3072, 768], replicated, may hold values from -0.109375 to 0.109375
- negative_ids: int32 [12288, 8], P('dp'), may hold values from 0 to 131071, as said below
Outputs:
- query_grad: bfloat16 [12288, 768], P(('dp', 'tower'))
- passage_grad: bfloat16 [12288, 768], P(('tower', 'dp'))
- negative_grad: bfloat16 [131072, 768], P(('tower', 'dp'))
Inputs may be any that keep to these rules, and one draw needn't show every extreme that they name: `negative_ids`: the owner of pool row r is the device with index r // 512 along tower+dp. Among the 1536 ids of one index of dp, at most 12 have one owner, and in every draw some owner gets exactly 12 of them; ids may repeat.
All inputs are finite; a program needn't handle non-finite values.
Results may differ from a plain program's by a relative error of at most 0.015.
Values may be sent and summed in bfloat16 or wider, within the bound.
A program may use at most 128 MiB of HBM per device.

v0:
```python
import jax
import jax.numpy as jnp
from jax import lax
from jax.sharding import PartitionSpec as P

logit_scale = 50.0


def unit_rows(hidden, weight):
    projected = jnp.dot(hidden, weight, preferred_element_type=jnp.float32)
    length = jnp.sqrt(jnp.sum(projected * projected, axis=1, keepdims=True) + 1e-06)
    return (projected / length).astype(jnp.bfloat16)


def shards(query_hidden, passage_hidden, pool_hidden, query_proj, passage_proj, negative_ids):
    tower_count = lax.axis_size("tower")
    dp_size = lax.axis_size("dp")
    tower_index = lax.axis_index("tower")
    dp_index = lax.axis_index("dp")
    query_count = query_hidden.shape[0]
    neg_count = negative_ids.shape[1]
    pool_rows = pool_hidden.shape[0]
    own_rows = passage_hidden.shape[0]
    block_rows = own_rows * dp_size
    cap_slots = 2 * query_count * neg_count // (tower_count * dp_size)
    slot_total = dp_size * cap_slots
    query_unit = unit_rows(query_hidden, query_proj)
    passage_unit = unit_rows(passage_hidden, passage_proj)
    pool_unit = unit_rows(pool_hidden, passage_proj)
    emb_width = query_unit.shape[1]
    passage_block = lax.all_gather(passage_unit, "dp", axis=0, tiled=True)
    scores = logit_scale * lax.dot_general(
        query_unit, passage_block, (((1,), (1,)), ((), ())), preferred_element_type=jnp.float32
    )
    exp_scores = jnp.exp(scores)
    pos_offset = dp_index * query_count - tower_index * block_rows
    has_pos = (pos_offset >= 0) & (pos_offset < block_rows)
    pos_start = jnp.clip(pos_offset, 0, block_rows - query_count)
    positives = lax.dynamic_slice_in_dim(passage_block, pos_start, query_count, 0)
    query_wide = query_unit.astype(jnp.float32)
    pos_score = logit_scale * jnp.sum(query_wide * positives.astype(jnp.float32), axis=1)
    pos_exp = jnp.where(has_pos, jnp.exp(pos_score), 0.0)
    flat_ids = negative_ids.reshape(-1)
    owner_index = flat_ids // pool_rows
    local_row = flat_ids % pool_rows
    in_tower = owner_index // dp_size == tower_index
    owner_rank = owner_index % dp_size
    member = ((owner_rank[:, None] == jnp.arange(dp_size)[None, :]) & in_tower[:, None]).astype(
        jnp.int32
    )
    before = jnp.cumsum(member, axis=0) - member
    slot_index = jnp.sum(before * member, axis=1)
    position = jnp.where(in_tower, owner_rank * cap_slots + slot_index, slot_total)
    requests = (
        jnp.zeros((slot_total,), jnp.int32)
        .at[position]
        .set(local_row, mode="drop")
        .reshape(dp_size, cap_slots)
    )
    asked_ids = lax.all_to_all(requests, "dp", split_axis=0, concat_axis=0, tiled=True)
    fetched = lax.all_to_all(pool_unit[asked_ids], "dp", split_axis=0, concat_axis=0, tiled=True)
    flat_fetched = fetched.reshape(slot_total, emb_width)
    entry_rows = flat_fetched[jnp.minimum(position, slot_total - 1)].reshape(
        query_count, neg_count, emb_width
    )
    neg_score = logit_scale * jnp.einsum(
        "qe,qke->qk", query_unit, entry_rows, preferred_element_type=jnp.float32
    )
    neg_exp = jnp.where(in_tower.reshape(query_count, neg_count), jnp.exp(neg_score), 0.0)
    batch_total, hard_total = lax.psum(
        (jnp.sum(exp_scores, axis=1), pos_exp + jnp.sum(neg_exp, axis=1)), "tower"
    )
    weights = (exp_scores / batch_total[:, None]).astype(jnp.bfloat16)
    pos_weight = pos_exp / hard_total
    hard_weight = neg_exp / hard_total[:, None]
    pos_coef = jnp.where(has_pos, pos_weight - 2.0, 0.0)
    query_term = logit_scale * (
        jnp.dot(weights, passage_block, preferred_element_type=jnp.float32)
        + pos_coef[:, None] * positives.astype(jnp.float32)
        + jnp.einsum("qk,qke->qe", hard_weight, entry_rows, preferred_element_type=jnp.float32)
    )
    query_grad = lax.psum_scatter(
        query_term.astype(jnp.bfloat16), "tower", scatter_dimension=0, tiled=True
    )
    pos_rows_coef = pos_coef[:, None] * query_wide
    product = lax.dot_general(
        weights, query_unit, (((0,), (0,)), ((), ())), preferred_element_type=jnp.float32
    )
    offsets = jnp.arange(own_rows * lax.axis_size("dp")) - pos_offset
    inside = (offsets >= 0) & (offsets < query_count)
    extra_rows = jnp.where(
        inside[:, None], pos_rows_coef[jnp.clip(offsets, 0, query_count - 1)], 0.0
    )
    passage_grad = lax.psum_scatter(
        logit_scale * (product + extra_rows), "dp", scatter_dimension=0, tiled=True
    ).astype(jnp.bfloat16)
    entry_grad = (logit_scale * hard_weight[:, :, None] * query_wide[:, None, :]).reshape(
        query_count * neg_count, emb_width
    )
    slot_grad = (
        jnp.zeros((slot_total, emb_width), jnp.float32)
        .at[position]
        .add(entry_grad, mode="drop")
        .reshape(dp_size, cap_slots, emb_width)
    )
    returned = lax.all_to_all(
        slot_grad.astype(jnp.bfloat16), "dp", split_axis=0, concat_axis=0, tiled=True
    ).astype(slot_grad.dtype)
    pool_grad = (
        jnp.zeros((pool_rows, emb_width), jnp.float32)
        .at[asked_ids.reshape(-1)]
        .add(returned.reshape(slot_total, emb_width))
    )
    return (query_grad, passage_grad, pool_grad.astype(jnp.bfloat16))


def solution(mesh):
    placed = (
        P("dp", None),
        P(("tower", "dp"), None),
        P(("tower", "dp"), None),
        P(),
        P(),
        P("dp", None),
    )
    return jax.shard_map(
        shards,
        mesh=mesh,
        in_specs=placed,
        out_specs=(P(("dp", "tower"), None), P(("tower", "dp"), None), P(("tower", "dp"), None)),
        check_vma=False,
    )
```

profile of v0, /device:TPU:24, one launch (start us, length us, event | category | flops | bytes accessed | tf_op | source)
XLA Modules:
  0.0 390.7 jit_solution(16382863483093785825)
XLA Ops:
  7.2 3.6 multiply_reduce_fusion.2
  10.8 0.7 divide_convert_fusion.3
  11.6 0.8 copy.15
  12.3 1.0 reshape.381
  13.3 1.0 reshape.380
  14.3 1.6 reshape.379
  16.0 0.8 fusion.17
  16.8 34.5 %reduce-window.6 = s32[64,12,128]{2,1,0:T(8,128)} reduce-window(s32[64,12,128]{2,1,0:T(8,128)} %fusion.17, s32[]{:T(128)} %constant.88.clone.1), window={size=1x1x128 pad=0_0x0_0x127_0}, to_apply=%region_6.7 | reduce-window | flops 12484608 | bytes 786436 | tf_op jit(solution)/shard_map/reduce-window
  51.3 2.0 slice.14
  53.4 1.3 copy.18
  54.7 0.6 reduce-window.9
  55.3 1.4 copy.19
  56.7 0.6 add_select_fusion
  57.3 1.2 broadcast_add_fusion
  58.7 1.4 fusion.40
  60.1 6.3 %scatter_custom_fusion = s32[768]{0:T(1024)S(1)} fusion(s32[1536]{0:T(1024)} %get-tuple-element.4, s32[1536]{0:T(1024)} %get-tuple-element.11, s32[]{:T(128)} %constant.88.clone.1), kind=kCustom, calls=%fused_computation.127 | custom fusion | bytes 3584 | tf_op jit(solution)/shard_map/scatter | solution.py:57
  66.5 0.7 all_to_all.14
  67.2 12.2 %all-to-all-start = ((s32[64,1,12]{2,1,0:T(1,128)}), s32[64,1,12]{2,1,0:T(1,128)}, u32[]{:S(2)}, u32[]{:S(2)}) async-start(s32[64,1,12]{2,1,0:T(1,128)} %bitcast.57), calls=%async_computation | async-start | bytes 65536 | tf_op jit(solution)/shard_map/all_to_all | solution.py:60
  79.4 6.0 %multiply_reduce_fusion = (f32[512]{0:T(512)S(1)}, f32[512,768]{1,0:T(8,128)S(1)}) fusion(bf16[512,3072]{1,0:T(8,128)(2,1)} %param.8, bf16[3072,768]{1,0:T(8,128)(2,1)} %param.10), kind=kOutput, calls=%fused_computation.19 | convolution fusion | flops 2416705024 | bytes 9439232 | tf_op jit(solution)/shard_map/dot_general | solution.py:10
  85.4 1.1 divide_convert_fusion.1
  86.5 2.3 all-to-all-done
  88.8 1.4 compare_select_fusion
  90.2 0.9 reshape.392
  91.1 5.2 %gather_fusion = bf16[768,768]{1,0:T(8,128)(2,1)} fusion(bf16[512,768]{1,0:T(8,128)(2,1)} %divide_convert_fusion.1, s32[1024]{0:T(1024)S(1)} %pad_clamp_fusion.1), kind=kCustom, calls=%fused_computation | custom fusion | bytes 2362368 | tf_op jit(solution)/shard_map/gather | solution.py:61
  96.3 3.1 reshape.391
  99.4 8.1 %all-to-all-start.1 = ((bf16[64,12,768]{2,1,0:T(8,128)(2,1)}), bf16[64,12,768]{2,1,0:T(8,128)(2,1)}, u32[]{:S(2)}, u32[]{:S(2)}) async-start(bf16[64,12,768]{2,1,0:T(8,128)(2,1)} %reshape.391), calls=%async_computation.1 | async-start | bytes 3145728 | tf_op jit(solution)/shard_map/all_to_all | solution.py:61
  107.8 0.6 fusion.24
  108.5 2.1 multiply_reduce_fusion.1
  110.6 0.6 broadcast_clamp_fusion
  111.2 1.1 fusion.51
  112.3 35.3 %all-to-all-done.1 = bf16[64,12,768]{2,1,0:T(8,128)(2,1)} async-done(((bf16[64,12,768]{2,1,0:T(8,128)(2,1)}), bf16[64,12,768]{2,1,0:T(8,128)(2,1)}, u32[]{:S(2)}, u32[]{:S(2)}) %all-to-all-start.1) | async-done | bytes 1179680 | tf_op jit(solution)/shard_map/all_to_all | solution.py:61
  147.6 3.1 reshape.383
  150.7 8.1 %gather_fusion.1 = bf16[1536,768]{1,0:T(8,128)(2,1)} fusion(bf16[768,768]{1,0:T(8,128)(2,1)} %reshape.383, s32[2048]{0:T(1024)S(1)} %pad_clamp_fusion), kind=kCustom, calls=%fused_computation.1 | custom fusion | bytes 4724736 | tf_op jit(solution)/shard_map/gather | solution.py:63
  158.9 3.6 fusion.4
  162.5 1.6 copy.23
  164.1 1.3 fusion.52
  165.3 1.2 fusion.14
  166.6 1.2 fusion.50
  167.8 6.1 %fusion.54 = (f32[192]{0:T(256)}, f32[192,3072]{1,0:T(8,128)}) fusion(bf16[192,768]{1,0:T(8,128)(2,1)} %get-tuple-element.8, bf16[3072,768]{1,0:T(8,128)(2,1)} %all-gather.2.cloned.1.call-done), kind=kOutput, calls=%fused_computation.137 | convolution fusion | flops 907149120 | bytes 7373568 | tf_op jit(solution)/shard_map/dot_general | solution.py:32
  173.9 8.1 %all-reduce = (f32[192]{0:T(256)S(1)}, f32[192]{0:T(256)}) all-reduce(f32[192]{0:T(256)} %fusion.50, f32[192]{0:T(256)} %get-tuple-element.19), channel_id=1, replica_groups=mesh['tower'=4,'dp'=64] {'tower'}, use_global_device_ids=true, to_apply=%region_11.12 | all-reduce | flops 384 | bytes 3072 | tf_op jit(solution)/shard_map/psum | solution.py:70
  182.1 0.6 copy-done.7
  182.6 1.9 broadcast_multiply_fusion
  184.5 17.1 %gather_fusion.2 = f32[3072,768]{1,0:T(8,128)} fusion(f32[192,768]{1,0:T(8,128)} %broadcast_multiply_fusion, s32[3072]{0:T(1024)} %broadcast_clamp_fusion), kind=kCustom, calls=%fused_computation.2 | custom fusion | bytes 18886656 | tf_op jit(solution)/shard_map/gather | solution.py:92
  201.6 8.2 %add_multiply_fusion = f32[3072,768]{1,0:T(8,128)} fusion(f32[3072,768]{1,0:T(8,128)} %gather_fusion.2, bf16[192,768]{1,0:T(8,128)(2,1)} %get-tuple-element.8, pred[3072]{0:T(1024)(128)(4,1)S(1)} %copy-done.4, f32[192,3072]{1,0:T(8,128)} %get-tuple-element.20, f32[192]{0:T(256)} %get-tuple-element.6), kind=kOutput, calls=%fused_computation.6 | convolution fusion | flops 914227200 | bytes 21532416 | tf_op jit(solution)/shard_map/dot_general | solution.py:86
  209.8 0.7 broadcast_multiply_fusion.1
  210.5 0.7 copy.21
  211.3 1.0 mul.128
  212.3 13.1 %scatter_custom_fusion.1 = f32[768,768]{1,0:T(8,128)} fusion(s32[1536]{0:T(1024)} %get-tuple-element.4, f32[192,768]{1,0:T(8,128)} %get-tuple-element.7, f32[1536]{0:T(1024)S(1)} %mul.128, f32[]{:T(128)} %constant.80.clone.1), kind=kCustom, calls=%fused_computation.8 | custom fusion | flops 2359296 | bytes 2955776 | tf_op jit(solution)/shard_map/scatter-add | solution.py:103
  225.3 2.9 convert_element_type.52
  228.2 3.2 convert_element_type.53
  231.5 5.5 %all-to-all-start.2 = ((bf16[64,12,768]{2,1,0:T(8,128)(2,1)}), bf16[64,12,768]{2,1,0:T(8,128)(2,1)}, u32[]{:S(2)}, u32[]{:S(2)}) async-start(bf16[64,12,768]{2,1,0:T(8,128)(2,1)} %convert_element_type.53), calls=%async_computation.4 | async-start | bytes 3145728 | tf_op jit(solution)/shard_map/all_to_all | solution.py:106
  237.3 0.8 copy.24
  238.1 2.7 fusion.2
  240.8 4.4 %fusion.10 = bf16[192,768]{1,0:T(8,128)(2,1)} fusion(bf16[3072,768]{1,0:T(8,128)(2,1)} %all-gather.2.cloned.1.call-done, f32[192,1,768]{2,1,0:T(1,128)S(1)} %fusion.2, f32[192]{0:T(256)} %copy-done.7, s32[]{:T(128)S(6)} %min.25, f32[192,3072]{1,0:T(8,128)S(1)} %copy-done.1, f32[192]{0:T(256)} %get-tuple-element.6), kind=kOutput, calls=%fused_computation.23 | convolution fusion | flops 908034048 | bytes 8259588 | tf_op jit(solution)/shard_map/dot_general | solution.py:78
  245.3 0.5 broadcast.570
  245.8 2.1 reduce.9
  247.9 0.9 reshape.385
  248.8 28.2 %all-to-all-done.2 = bf16[64,12,768]{2,1,0:T(8,128)(2,1)} async-done(((bf16[64,12,768]{2,1,0:T(8,128)(2,1)}), bf16[64,12,768]{2,1,0:T(8,128)(2,1)}, u32[]{:S(2)}, u32[]{:S(2)}) %all-to-all-start.2) | async-done | bytes 1179680 | tf_op jit(solution)/shard_map/all_to_all | solution.py:106
  277.0 3.2 reshape.434
  280.2 9.3 %scatter_custom_fusion.2 = f32[512,768]{1,0:T(8,128)} fusion(s32[768]{0:T(1024)S(1)} %fusion.46, f32[768,768]{1,0:T(8,128)} %reshape.434, f32[]{:T(128)} %constant.80.clone.1), kind=kCustom, calls=%fused_computation.25 | custom fusion | flops 589824 | bytes 1573376 | tf_op jit(solution)/shard_map/scatter-add | solution.py:112
  289.5 2.4 convert_element_type.54
  291.8 69.6 %reduce-scatter.5.cloned.1.call-done = f32[48,768]{1,0:T(8,128)} async-done(((f32[3072,768]{1,0:T(8,128)}), f32[48,768]{1,0:T(8,128)}) %reduce-scatter.5.cloned.1.call-update) | async-done | bytes 147472 | tf_op jit(solution)/shard_map/reduce_scatter | solution.py:94
  361.5 1.6 convert_element_type.51
  363.0 21.2 %reduce-scatter.3.cloned.1.call-done = bf16[48,768]{1,0:T(8,128)(2,1)} async-done(((bf16[192,768]{1,0:T(8,128)(2,1)}), bf16[48,768]{1,0:T(8,128)(2,1)}) %reduce-scatter.3.cloned.1.call-update) | async-done | bytes 73744 | tf_op jit(solution)/shard_map/reduce_scatter | solution.py:82
  (35 shorter events, 0.9 us)
Async XLA Ops:
  7.2 101.3 %copy-start = (bf16[2304,768]{1,0:T(8,128)(2,1)S(1)}, bf16[2304,768]{1,0:T(8,128)(2,1)}, u32[]{:S(2)}) copy-start(bf16[2304,768]{1,0:T(8,128)(2,1)} %param.9) | copy-start | bytes 10616836
  7.2 4.4 %copy-start.2 = (s32[192,8]{0,1:T(8,128)S(1)}, s32[192,8]{0,1:T(8,128)}, u32[]{:S(2)}) copy-start(s32[192,8]{0,1:T(8,128)} %param.11) | copy-start | bytes 18436
  7.2 158.2 %all-gather.2.cloned.1.call-start = ((), (), s32[]{:S(2)}) async-start(), calls=%async_computation.5 | async-start | bytes 4792320 | tf_op jit(solution)/shard_map/all_gather | solution.py:31
  67.2 21.7 %all-to-all-start = ((s32[64,1,12]{2,1,0:T(1,128)}), s32[64,1,12]{2,1,0:T(1,128)}, u32[]{:S(2)}, u32[]{:S(2)}) async-start(s32[64,1,12]{2,1,0:T(1,128)} %bitcast.57), calls=%async_computation | async-start | bytes 65536 | tf_op jit(solution)/shard_map/all_to_all | solution.py:60
  99.4 48.2 %all-to-all-start.1 = ((bf16[64,12,768]{2,1,0:T(8,128)(2,1)}), bf16[64,12,768]{2,1,0:T(8,128)(2,1)}, u32[]{:S(2)}, u32[]{:S(2)}) async-start(bf16[64,12,768]{2,1,0:T(8,128)(2,1)} %reshape.391), calls=%async_computation.1 | async-start | bytes 3145728 | tf_op jit(solution)/shard_map/all_to_all | solution.py:61
  107.6 253.9 %reduce-scatter.5.cloned.1.call-start = ((), (), s32[]{:S(2)}) async-start(), calls=%async_computation.7 | async-start | bytes 9584640 | tf_op jit(solution)/shard_map/reduce_scatter | solution.py:94
  158.9 5.2 %copy-start.3 = (s32[192,8]{0,1:T(8,128)S(1)}, s32[192,8]{0,1:T(8,128)}, u32[]{:S(2)}) copy-start(s32[192,8]{0,1:T(8,128)} %param.11) | copy-start | bytes 18436
  182.0 19.6 %copy-start.5 = (f32[192]{0:T(256)}, f32[192]{0:T(256)S(1)}, u32[]{:S(2)}) copy-start(f32[192]{0:T(256)S(1)} %get-tuple-element.5) | copy-start | bytes 2308
  182.1 0.6 copy-start.7
  184.5 17.1 %copy-start.4 = (pred[3072]{0:T(1024)(128)(4,1)S(1)}, pred[3072]{0:T(1024)(128)(4,1)}, u32[]{:S(2)}) copy-start(pred[3072]{0:T(1024)(128)(4,1)} %fusion.24) | copy-start | bytes 9220
  228.2 9.0 %copy-start.6 = (f32[192]{0:T(256)S(1)}, f32[192]{0:T(256)}, u32[]{:S(2)}) copy-start(f32[192]{0:T(256)} %copy-done.5) | copy-start | bytes 2308
  231.5 45.5 %all-to-all-start.2 = ((bf16[64,12,768]{2,1,0:T(8,128)(2,1)}), bf16[64,12,768]{2,1,0:T(8,128)(2,1)}, u32[]{:S(2)}, u32[]{:S(2)}) async-start(bf16[64,12,768]{2,1,0:T(8,128)(2,1)} %convert_element_type.53), calls=%async_computation.4 | async-start | bytes 3145728 | tf_op jit(solution)/shard_map/all_to_all | solution.py:106
  237.0 147.2 %reduce-scatter.3.cloned.1.call-start = ((), (), s32[]{:S(2)}) async-start(), calls=%async_computation.6 | async-start | bytes 368640 | tf_op jit(solution)/shard_map/reduce_scatter | solution.py:82
  238.1 2.7 copy-start.1
Sparse Core Ops, SparseCore 0:
  11.7 82.3 all-gather.1
  209.9 151.4 reduce-scatter.4
  364.6 19.5 reduce-scatter.2
where the time goes:
time: 397 us; the launch traced here: 391 us
  waiting for transfers between devices  157 us (40%)
  other arithmetic  82.6 us (21%)
  local copies, waits for them, and re-layouts  66.1 us (17%)
  matrix products  36.8 us (9%)
  starting transfers between devices  26.4 us (7%)
  between operations  14 us (4%)
  blocking collectives  8.14 us (2%)
    reduce_scatter x1, waiting for transfers between devices, shards(): lax.psum_scatter(logit_scale * (product + extra_rows), 'dp', scatter_dime...  69.6 us
    another operation x3, other arithmetic  36.4 us
    all_to_all x1, waiting for transfers between devices, shards(): lax.all_to_all(pool_unit[asked_ids], 'dp', split_axis=0, concat_axis=0, t...  35.3 us
    all_to_all x1, waiting for transfers between devices, shards(): lax.all_to_all(slot_grad.astype(jnp.bfloat16), 'dp', split_axis=0, concat...  28.2 us
    reduce_scatter x1, waiting for transfers between devices, shards(): lax.psum_scatter(query_term.astype(jnp.bfloat16), 'tower', scatter_dimens...  21.2 us
    gather x1, local copies, waits for them, and re-layouts, shards(): pos_rows_coef[jnp.clip(offsets, 0, query_count - 1)]  17.1 us
    scatter-add x1, other arithmetic, shards(): slot_grad = jnp.zeros((slot_total, emb_width), jnp.float32).at[position]....  13.1 us
    all_to_all x1, starting transfers between devices, shards(): lax.all_to_all(requests, 'dp', split_axis=0, concat_axis=0, tiled=True)  12.2 us
  transfers between devices with their start and end apart: 6, of which 5 were waited for; matrix products, arithmetic and copies ran while one was open for 37% of the time, Pallas kernels for 0%

commit v1 on v0

v1 whole, which is shorter than its diff:
```python
import functools

import jax
import jax.numpy as jnp
from jax import lax
from jax.experimental import pallas as pl
from jax.experimental.pallas import tpu as pltpu
from jax.sharding import PartitionSpec as P

logit_scale = 50.0
MESH = pl.DeviceIdType.MESH
NY, NZ, NX, NC = 4, 8, 4, 2
PLANE = NY * NX * NC
F32 = jnp.float32
BF16 = jnp.bfloat16


def place():
    y = lax.axis_index("tower")
    dp = lax.axis_index("dp")
    return y, dp, dp // 8, (dp // 2) % 4, dp % 2


class Route:
    def __init__(self, count, dest, source, slot, own, item=None):
        self.count, self.dest, self.source = count, dest, source
        self.slot, self.own, self.item = slot, own, item


def routes():
    y, dp, z, x, c = place()
    line = x * 2 + c
    member, chip, core_line = y * 8 + line, y * 4 + x, z * 2 + c
    sibling = dp + 1 - 2 * c
    lead = (z % 2) * 4 + y
    at_home = z // 2 == y

    def around(base, i, n):
        return lax.rem(base + i, n)

    def plane(i):
        m = around(member, i, 32)
        return m // 8, z * 8 + m % 8

    def plane_core(i):
        n = around(chip, i, 16)
        return n // 4, z * 8 + (n % 4) * 2 + c

    def zcore(i):
        g = around(core_line, i, 16)
        return y, (g // 2) * 8 + x * 2 + g % 2

    def holder(i):
        return z // 2, around(z, i, 8) * 8 + line

    def home(i):
        k = around(lead, i, 8)
        return k % 4, (2 * y + k // 4) * 8 + line

    perm_e = (dp % 4, y * 16 + dp // 4)
    perm_f = (dp // 16, (dp % 16) * 4 + y)
    perm_own = (dp % 4 == y) & (y * 16 + dp // 4 == dp)
    perm_f_own = (dp // 16 == y) & ((dp % 16) * 4 + y == dp)
    return {
        "plane": Route(32, plane, plane, member, "yes", lambda i: around(member, i, 32)),
        "plane_core": Route(16, plane_core, plane_core, chip, "yes", lambda i: around(chip, i, 16)),
        "zline": Route(8, lambda i: (y, around(z, i, 8) * 8 + line), lambda i: (y, around(z, i, 8) * 8 + line), z, "yes"),
        "zcore": Route(16, zcore, zcore, core_line, "yes"),
        "holder": Route(8, holder, home, lead, at_home),
        "home": Route(8, home, holder, z, at_home, lambda i: around(lead, i, 8)),
        "sibling": Route(1, lambda i: (y, sibling), lambda i: (y, sibling), 0, None),
        "to_query": Route(1, lambda i: perm_e, lambda i: perm_f, 0, perm_own),
        "to_passage": Route(1, lambda i: perm_f, lambda i: perm_e, 0, perm_f_own),
    }


def loop(lo, hi, body):
    def step(i, carry):
        body(i)
        return carry

    lax.fori_loop(lo, hi, step, 0)


def enter(names, table):
    barrier = pltpu.get_barrier_semaphore()
    wanted = 0
    for name in names:
        route = table[name]

        def greet(i, route=route):
            ty, td = route.source(i)
            pl.semaphore_signal(barrier, inc=1, device_id=(ty, td), device_id_type=MESH)

        if route.own is None:
            greet(0)
            wanted = wanted + 1
            continue
        if route.own == "yes" if isinstance(route.own, str) else False:
            loop(1, route.count, greet)
            wanted = wanted + route.count - 1
            continue

        @pl.when(jnp.logical_not(route.own))
        def _(greet=greet):
            greet(0)

        if route.count > 1:
            loop(1, route.count, greet)
        wanted = wanted + route.count - 1 + jnp.where(route.own, 0, 1)
    pl.semaphore_wait(barrier, wanted)


class Transfer:
    def __init__(self, route, src, dst, send_sem, recv_sem):
        self.route, self.src, self.dst = route, src, dst
        self.send_sem, self.recv_sem = send_sem, recv_sem

    def copy(self, i):
        ty, td = self.route.dest(i)
        slot = self.route.slot
        return pltpu.make_async_remote_copy(
            src_ref=self.src(i),
            dst_ref=self.dst(slot),
            send_sem=self.send_sem.at[i],
            recv_sem=self.recv_sem.at[slot],
            device_id=(ty, td),
            device_id_type=MESH,
        )

    def local(self):
        slot = self.route.slot
        return pltpu.make_async_copy(self.src(0), self.dst(slot), self.recv_sem.at[slot])

    def each(self, far, near):
        own = self.route.own
        if own is None:
            far(0)
        elif isinstance(own, str):
            near()
        else:

            @pl.when(own)
            def _():
                near()

            @pl.when(jnp.logical_not(own))
            def _():
                far(0)

        if self.route.count > 1:
            loop(1, self.route.count, far)

    def start(self):
        self.each(lambda i: self.copy(i).start(), lambda: self.local().start())

    def wait_slot(self, k):
        pltpu.make_async_copy(self.dst(k), self.dst(k), self.recv_sem.at[k]).wait()

    def wait_recv(self):
        if self.route.count == 1:
            self.wait_slot(0)
        else:
            loop(0, self.route.count, self.wait_slot)

    def wait_send(self):
        self.each(lambda i: self.copy(i).wait_send(), lambda: None)


def sems(n):
    return [pltpu.SemaphoreType.DMA((n,)), pltpu.SemaphoreType.DMA((n,))]


def call(kernel, outs, counts, ident, args):
    return pl.pallas_call(
        kernel,
        out_shape=[jax.ShapeDtypeStruct(s, d) for s, d in outs],
        in_specs=[pl.BlockSpec(memory_space=pl.ANY)] * len(args),
        out_specs=[pl.BlockSpec(memory_space=pl.ANY)] * len(outs),
        scratch_shapes=sum([sems(n) for n in counts], []),
        compiler_params=pltpu.CompilerParams(collective_id=ident, has_side_effects=True),
        name="exchange_%d" % ident,
    )(*args)


def run(transfers):
    for t in transfers:
        t.start()
    for t in transfers:
        t.wait_recv()
    for t in transfers:
        t.wait_send()


def spread_kernel(q, p, ids, qh, ph, idh, pp, qq, s0, r0, s1, r1, s2, r2, s3, r3, s4, r4, s5, r5):
    table = routes()
    y, dp, z, x, c = place()
    enter(["holder", "plane_core", "to_query", "to_passage", "sibling"], table)
    hold = Transfer(table["holder"], lambda i: q, lambda k: qh.at[c, k], s0, r0)
    hold_ids = Transfer(table["holder"], lambda i: ids, lambda k: idh.at[k], s1, r1)
    pass_on = Transfer(table["plane_core"], lambda i: p, lambda k: ph.at[k], s2, r2)
    pair_p = Transfer(table["to_query"], lambda i: p, lambda k: pp, s3, r3)
    pair_q = Transfer(table["to_passage"], lambda i: q, lambda k: qq, s4, r4)
    for t in (hold_ids, hold, pass_on, pair_p, pair_q):
        t.start()

    def forward(k):
        return pltpu.make_async_remote_copy(
            src_ref=qh.at[c, k],
            dst_ref=qh.at[c, k],
            send_sem=s5.at[k],
            recv_sem=r5.at[k],
            device_id=(y, dp + 1 - 2 * c),
            device_id_type=MESH,
        )

    def hand(k):
        hold.wait_slot(k)
        forward(k).start()

    loop(0, 8, hand)

    def taken(k):
        pltpu.make_async_copy(qh.at[1 - c, k], qh.at[1 - c, k], r5.at[k]).wait()

    loop(0, 8, taken)
    for t in (hold_ids, pass_on, pair_p, pair_q):
        t.wait_recv()
    for t in (hold_ids, hold, pass_on, pair_p, pair_q):
        t.wait_send()
    loop(0, 8, lambda k: forward(k).wait_send())


def ask_kernel(xs, rows, sums, pos, xo, rowo, sumo, poso, s0, r0, s1, r1, s2, r2, s3, r3):
    table = routes()
    enter(["plane", "zcore", "holder"], table)
    plane = table["plane"]
    run(
        [
            Transfer(table["zcore"], lambda i: sums, lambda k: sumo.at[k], s2, r2),
            Transfer(table["holder"], lambda i: pos, lambda k: poso.at[k], s3, r3),
            Transfer(plane, lambda i: rows.at[plane.item(i)], lambda k: rowo.at[k], s1, r1),
            Transfer(plane, lambda i: xs.at[plane.item(i)], lambda k: xo.at[k], s0, r0),
        ]
    )


def answer_kernel(ys, es, part, yo, eo, parto, s0, r0, s1, r1, s2, r2):
    table = routes()
    enter(["plane", "sibling"], table)
    plane = table["plane"]
    run(
        [
            Transfer(plane, lambda i: es.at[plane.item(i)], lambda k: eo.at[k], s1, r1),
            Transfer(table["sibling"], lambda i: part, lambda k: parto, s2, r2),
            Transfer(plane, lambda i: ys.at[plane.item(i)], lambda k: yo.at[k], s0, r0),
        ]
    )


def total_kernel(tot, line, homes, s0, r0, s1, r1):
    table = routes()
    enter(["zline", "home"], table)
    run(
        [
            Transfer(table["zline"], lambda i: tot, lambda k: line.at[k], s0, r0),
            Transfer(table["home"], lambda i: tot, lambda k: homes.at[k], s1, r1),
        ]
    )


def finish_kernel(zs, inv, gs, pw, zo, invo, go, pwo, s0, r0, s1, r1, s2, r2, s3, r3):
    table = routes()
    enter(["home", "plane", "plane_core", "to_passage"], table)
    home, plane, core = table["home"], table["plane"], table["plane_core"]
    run(
        [
            Transfer(plane, lambda i: inv.at[plane.item(i)], lambda k: invo.at[k], s1, r1),
            Transfer(table["to_passage"], lambda i: pw, lambda k: pwo, s3, r3),
            Transfer(home, lambda i: zs.at[home.item(i)], lambda k: zo.at[k], s0, r0),
            Transfer(core, lambda i: gs.at[core.item(i)], lambda k: go.at[k], s2, r2),
        ]
    )


def unit_rows(hidden, weight):
    projected = jnp.dot(hidden, weight, preferred_element_type=F32)
    length = jnp.sqrt(jnp.sum(projected * projected, axis=1, keepdims=True) + 1e-06)
    return (projected / length).astype(BF16)


def lanes(values):
    lead, n = values.shape[:-1], values.shape[-1]
    rows = -(-n // 128)
    values = jnp.pad(values, [(0, 0)] * len(lead) + [(0, rows * 128 - n)])
    values = values.reshape(lead + (rows, 128))
    return jnp.pad(values, [(0, 0)] * len(lead) + [(0, 8 - rows), (0, 0)])


def shards(query_hidden, passage_hidden, pool_hidden, query_proj, passage_proj, negative_ids):
    y, dp, z, x, c = place()
    emb = query_proj.shape[1]
    cap = 12
    own_hidden = lax.dynamic_slice_in_dim(query_hidden, y * 48, 48, 0)
    own_ids = lax.dynamic_slice_in_dim(negative_ids, y * 48, 48, 0)
    q48 = unit_rows(own_hidden, query_proj)
    p48 = unit_rows(passage_hidden, passage_proj)
    pool = unit_rows(pool_hidden, passage_proj)
    ids48 = jnp.pad(own_ids.T, ((0, 0), (0, 80)))

    qh, ph, idh, pp, qq = call(
        spread_kernel,
        [((2, 8, 48, emb), BF16), ((16, 48, emb), BF16), ((8, 8, 128), jnp.int32), ((48, emb), BF16), ((48, emb), BF16)],
        [8, 8, 16, 1, 1, 8],
        1,
        [q48, p48, ids48],
    )
    q_all = qh.reshape(768, emb)
    q_own = lax.dynamic_index_in_dim(qh, c, 0, keepdims=False).reshape(384, emb)
    p_all = ph.reshape(768, emb)

    ids = idh[:, :, :48].reshape(2, 4, 8, 48).transpose(0, 2, 1, 3).reshape(2, 8, 192)
    owner, local_row = ids // 512, ids % 512
    in_plane = (owner // 8) % 8 == z
    target = jnp.where(in_plane, (owner // 64) * 8 + owner % 8, -1)
    names = (target[:, :, None, :] == jnp.arange(PLANE, dtype=jnp.int32)[None, None, :, None]).astype(F32)
    per_query = jnp.sum(names, axis=1)
    before = (jnp.arange(192)[:, None] < jnp.arange(192)[None, :]).astype(BF16)
    earlier = lax.dot_general(
        per_query.astype(BF16).reshape(2 * PLANE, 192), before, (((1,), (0,)), ((), ())), preferred_element_type=F32
    ).reshape(2, PLANE, 192)
    ranks = []
    running = earlier
    for k in range(8):
        ranks.append(jnp.sum(names[:, k] * running, axis=1))
        running = running + names[:, k]
    rank = jnp.stack(ranks, axis=1).astype(jnp.int32)
    half = jnp.arange(2, dtype=jnp.int32)[:, None, None]
    slot = jnp.where(in_plane, target * (2 * cap) + half * cap + rank, -1)
    slot = slot.transpose(1, 0, 2).reshape(8, 384)
    row_code = (local_row + 1).transpose(1, 0, 2).reshape(8, 384)
    slot_ids = jnp.arange(PLANE * 2 * cap, dtype=jnp.int32)[:, None]
    pick = jnp.zeros((768, 384), F32)
    for k in range(8):
        hit = slot[k][None, :] == slot_ids
        pick = jnp.where(hit, 1.0, pick)
    pick = pick.astype(BF16)
    row_of = jnp.sum(
        sum(jnp.where(slot[k][None, :] == slot_ids, row_code[k][None, :], 0) for k in range(8)), axis=1
    )
    asked = jnp.dot(pick, q_own, preferred_element_type=F32).astype(BF16)

    scores = logit_scale * lax.dot_general(q_all, p_all, (((1,), (1,)), ((), ())), preferred_element_type=F32)
    exp_scores = jnp.exp(scores)
    row_sums = jnp.sum(exp_scores, axis=1)
    exp_low = exp_scores.astype(BF16)
    pos_exp = jnp.exp(logit_scale * jnp.sum(q48.astype(F32) * pp.astype(F32), axis=1))

    xo, rowo, sumo, poso = call(
        ask_kernel,
        [((32, 24, emb), BF16), ((32, 8, 128), jnp.int32), ((16, 8, 128), F32), ((8, 8, 128), F32)],
        [32, 32, 16, 8],
        2,
        [asked.reshape(32, 24, emb), lanes(row_of.reshape(32, 24)), lanes(row_sums), lanes(pos_exp)],
    )
    x_rows = xo.reshape(768, emb)
    row_code_o = rowo[:, 0, :24].reshape(768)
    chosen = (row_code_o[None, :] == jnp.arange(1, 513, dtype=jnp.int32)[:, None]).astype(BF16)
    named = lax.dot_general(chosen, pool, (((0,), (0,)), ((), ())), preferred_element_type=F32)
    neg_exp = jnp.exp(logit_scale * jnp.sum(x_rows.astype(F32) * named, axis=1))
    weighted = (neg_exp[:, None] * named).astype(BF16)

    inv_batch = 1.0 / jnp.sum(sumo, axis=0)[:6].reshape(768)
    query_part = jnp.dot(exp_low, p_all, preferred_element_type=F32).reshape(2, 384, emb)
    mine = lax.dynamic_index_in_dim(query_part, c, 0, keepdims=False)
    theirs = lax.dynamic_index_in_dim(query_part, 1 - c, 0, keepdims=False).astype(BF16)
    scaled_q = (q_all.astype(F32) * inv_batch[:, None]).astype(BF16)
    passage_part = lax.dot_general(exp_low, scaled_q, (((0,), (0,)), ((), ())), preferred_element_type=F32)

    yo, eo, sib = call(
        answer_kernel,
        [((32, 24, emb), BF16), ((32, 8, 128), F32), ((384, emb), BF16)],
        [32, 32, 1],
        3,
        [weighted.reshape(32, 24, emb), lanes(neg_exp.reshape(32, 24)), theirs],
    )
    hard_rows = lax.dot_general(pick, yo.reshape(768, emb), (((0,), (0,)), ((), ())), preferred_element_type=F32)
    neg_total = jnp.dot(
        eo[:, 0, :24].reshape(1, 768), pick.astype(F32), precision=lax.Precision.HIGHEST, preferred_element_type=F32
    ).reshape(384)

    line, homes = call(
        total_kernel, [((8, 8, 128), F32), ((8, 8, 128), F32)], [8, 8], 4, [lanes(neg_total)]
    )
    pos_held = poso[:, 0, :48].reshape(384)
    inv_hard = 1.0 / (jnp.sum(line, axis=0)[:3].reshape(384) + pos_held)
    inv_own = lax.dynamic_index_in_dim(inv_batch.reshape(2, 384), c, 0, keepdims=False)
    query_sum = (
        (mine + sib.astype(F32)) * inv_own[:, None] + hard_rows * inv_hard[:, None]
    ).astype(BF16)
    inv_slots = jnp.dot(
        inv_hard.reshape(1, 384), pick.astype(F32).T, precision=lax.Precision.HIGHEST, preferred_element_type=F32
    ).reshape(32, 24)
    home_total = jnp.sum(homes, axis=0)[:3].reshape(8, 48)
    home_total = lax.dynamic_index_in_dim(home_total, (z % 2) * 4 + y, 0, keepdims=False)
    pos_coef = pos_exp / (pos_exp + home_total) - 2.0

    zo, invo, go, pwo = call(
        finish_kernel,
        [((8, 48, emb), BF16), ((32, 8, 128), F32), ((16, 48, emb), BF16), ((8, 128), F32)],
        [8, 32, 16, 1],
        5,
        [query_sum.reshape(8, 48, emb), lanes(inv_slots), passage_part.astype(BF16).reshape(16, 48, emb), lanes(pos_coef)],
    )
    query_grad = logit_scale * (jnp.sum(zo.astype(F32), axis=0) + pos_coef[:, None] * pp.astype(F32))
    passage_grad = logit_scale * (jnp.sum(go.astype(F32), axis=0) + pwo[0, :48][:, None] * qq.astype(F32))
    hard_weight = neg_exp * invo[:, 0, :24].reshape(768)
    spread = (chosen.astype(F32) * hard_weight[None, :]).astype(BF16)
    negative_grad = logit_scale * jnp.dot(spread, x_rows, preferred_element_type=F32)
    return query_grad.astype(BF16), passage_grad.astype(BF16), negative_grad.astype(BF16)


def solution(mesh):
    placed = (
        P("dp", None),
        P(("tower", "dp"), None),
        P(("tower", "dp"), None),
        P(),
        P(),
        P("dp", None),
    )
    return jax.shard_map(
        shards,
        mesh=mesh,
        in_specs=placed,
        out_specs=(P(("dp", "tower"), None), P(("tower", "dp"), None), P(("tower", "dp"), None)),
        check_vma=False,
    )
```

time: 397 us -> 267 us (0.67); the launches traced: 391 us -> 265 us
  waiting for transfers between devices: 157 us -> 0 us
  Pallas kernels: 0 us -> 151 us
  other arithmetic: 82.6 us -> 18.7 us
  starting transfers between devices: 26.4 us -> 0 us
  between operations: 14 us -> 1.28 us
  blocking collectives: 8.14 us -> 0 us
  local copies, waits for them, and re-layouts: 66.1 us -> 59.3 us
    pallas_call x0 -> x5, Pallas kernels: none -> 151 us  [call(): pl.pallas_call(kernel, out_shape=[jax.ShapeDtypeStruct(s, d) for s, d in...]
    reduce_scatter x2 -> x0, waiting for transfers between devices: 90.8 us -> none  [the longest x1 69.6 us: shards(): lax.psum_scatter(logit_scale * (product + extra_rows), 'dp', scatter_dime...]
    all_to_all x3 -> x0, waiting for transfers between devices: 65.9 us -> none  [the longest x1 35.3 us: shards(): lax.all_to_all(pool_unit[asked_ids], 'dp', split_axis=0, concat_axis=0, t...]
    another operation x3 -> x0, other arithmetic: 36.4 us -> none
    gather x4 -> x0, local copies, waits for them, and re-layouts: 33.6 us -> none  [the longest x1 17.1 us: shards(): pos_rows_coef[jnp.clip(offsets, 0, query_count - 1)]]
    all_to_all x3 -> x0, starting transfers between devices: 25.9 us -> none  [the longest x1 12.2 us: shards(): lax.all_to_all(requests, 'dp', split_axis=0, concat_axis=0, tiled=True)]
    scatter-add x2 -> x0, other arithmetic: 22.3 us -> none  [the longest x1 13.1 us: shards(): slot_grad = jnp.zeros((slot_total, emb_width), jnp.float32).at[position]....]
    eq x0 -> x17, local copies, waits for them, and re-layouts: none -> 14.9 us  [the longest x16 14.2 us: shards(): hit = slot[k][None, :] == slot_ids]
  transfers between devices with their start and end apart: 6 -> 0, of which waited for: 5 -> 0; matrix products, arithmetic and copies ran while one was open for 37% -> 0% of each run, Pallas kernels for 0% -> 0%
where the time goes in v1:
time: 267 us; the launch traced here: 265 us
  Pallas kernels  151 us (57%)
  local copies, waits for them, and re-layouts  59.3 us (22%)
  matrix products  35.1 us (13%)
  other arithmetic  18.7 us (7%)
    pallas_call x5, Pallas kernels, call(): pl.pallas_call(kernel, out_shape=[jax.ShapeDtypeStruct(s, d) for s, d in...  151 us
    eq x16, local copies, waits for them, and re-layouts, shards(): hit = slot[k][None, :] == slot_ids  14.2 us
    broadcast_in_dim x8, local copies, waits for them, and re-layouts, shards(): jnp.where(slot[k][None, :] == slot_ids, row_code[k][None, :], 0)  10.6 us
    dot_general x3, matrix products, unit_rows(): projected = jnp.dot(hidden, weight, preferred_element_type=F32)  9.19 us
    another operation x9, local copies, waits for them, and re-layouts, shards(): rank = jnp.stack(ranks, axis=1).astype(jnp.int32)  5.43 us

profile of v1, /device:TPU:24, one launch (start us, length us, event | category | flops | bytes accessed | tf_op | source)
XLA Modules:
  0.0 265.0 jit_solution(6157346463388562510)
XLA Ops:
  1.9 0.8 dynamic-slice_bitcast_fusion
  3.8 1.9 multiply_reduce_fusion.3
  6.4 0.7 divide_convert_fusion.3.q
  7.2 3.5 %multiply_reduce_fusion.2 = (f32[48]{0:T(128)S(1)}, f32[48,768]{1,0:T(8,128)S(1)}) fusion(bf16[48,3072]{1,0:T(8,128)(2,1)S(1)} %copy-done.7, bf16[3072,768]{1,0:T(8,128)(2,1)} %param.10), kind=kOutput, calls=%fused_computation.70 | convolution fusion | flops 226566096 | bytes 5161152 | tf_op jit(solution)/shard_map/dot_general | solution.py:287
  10.7 0.7 divide_convert_fusion.2.p
  11.4 3.8 %multiply_reduce_fusion.1 = (f32[512]{0:T(512)S(1)}, f32[512,768]{1,0:T(8,128)}) fusion(bf16[512,3072]{1,0:T(8,128)(2,1)S(1)} %copy-done.40, bf16[3072,768]{1,0:T(8,128)(2,1)S(1)} %copy-done.1), kind=kOutput, calls=%fused_computation.13 | convolution fusion | flops 2416705024 | bytes 9439232 | tf_op jit(solution)/shard_map/dot_general | solution.py:287
  15.8 33.3 %exchange_1.1 = (bf16[2,8,48,768]{3,2,1,0:T(8,128)(2,1)}, bf16[16,48,768]{2,1,0:T(8,128)(2,1)}, s32[8,8,128]{2,1,0:T(8,128)}, bf16[48,768]{1,0:T(8,128)(2,1)}, bf16[48,768]{1,0:T(8,128)(2,1)}) custom-call(bf16[48,768]{1,0:T(8,128)(2,1)} %divide_convert_fusion.3.q, bf16[48,768]{1,0:T(8,128)(2,1)} %divide_convert_fusion.2.p, s32[8,128]{1,0:T(8,128)} %pad.48.ids), custom_call_target="tpu_custom_call" | custom-call | tf_op jit(solution)/shard_map/exchange_1/pallas_call | solution.py:175
  49.1 1.7 fusion.26
  50.8 1.4 copy.17
  52.2 0.8 reshape.495
  56.2 1.3 broadcast_in_dim.113
  57.6 1.3 broadcast_in_dim.128
  58.9 1.3 broadcast_in_dim.126
  60.2 1.3 broadcast_in_dim.124
  61.6 1.3 broadcast_in_dim.122
  62.9 1.3 broadcast_in_dim.120
  64.2 1.3 broadcast_in_dim.118
  65.5 1.3 broadcast_in_dim.116
  71.9 0.8 stack.35
  72.7 0.8 select_bitcast_fusion
  74.1 1.3 eq.500
  75.5 1.3 eq.536
  76.8 1.3 eq.528
  78.1 1.3 eq.564
  79.4 1.3 eq.524
  80.8 1.3 eq.560
  82.1 1.3 eq.520
  83.4 1.3 eq.556
  87.7 2.4 add_reduce_fusion
  90.7 0.8 reshape.498
  92.3 1.1 constant_dynamic-slice_fusion.2
  93.5 2.5 convolution_convert_fusion.1
  95.9 2.2 fusion.1
  98.7 31.5 %exchange_2.1 = (bf16[32,24,768]{2,1,0:T(8,128)(2,1)}, s32[32,8,128]{2,1,0:T(8,128)}, f32[16,8,128]{2,1,0:T(8,128)}, f32[8,8,128]{2,1,0:T(8,128)}) custom-call(bf16[32,24,768]{2,1,0:T(8,128)(2,1)} %bitcast.156, s32[32,8,128]{2,1,0:T(8,128)} %pad.50.rows, f32[8,128]{1,0:T(8,128)} %pad.51.sums, f32[8,128]{1,0:T(8,128)} %pad.53.pos), custom_call_target="tpu_custom_call" | custom-call | tf_op jit(solution)/shard_map/exchange_2/pallas_call | solution.py:175
  130.2 0.9 slice_reduce_fusion.2
  131.2 0.7 eq.532
  131.9 0.9 reduce_sum.205
  132.7 3.9 %convolution_convert_fusion = bf16[768,768]{1,0:T(8,128)(2,1)} fusion(bf16[768,768]{1,0:T(8,128)(2,1)} %get-tuple-element.72, bf16[768,768]{1,0:T(8,128)(2,1)} %bitcast.160, f32[768]{0:T(1024)S(1)} %get-tuple-element.77), kind=kOutput, calls=%fused_computation.14 | convolution fusion | flops 908328960 | bytes 3542016 | tf_op jit(solution)/shard_map/dot_general | solution.py:378
  137.3 0.8 fusion.70
  139.4 2.9 %multiply_reduce_fusion = (f32[768]{0:T(1024)S(1)}, f32[768,768]{1,0:T(8,128)S(1)}) fusion(bf16[32,24,768]{2,1,0:T(8,128)(2,1)} %get-tuple-element.25, f32[512,768]{1,0:T(8,128)} %get-tuple-element.80, f32[512]{0:T(512)} %add_sqrt_fusion, s32[768]{0:T(1024)S(1)} %copy-done.35, s32[512]{0:T(512)S(1)} %copy-done.38), kind=kOutput, calls=%fused_computation.3 | convolution fusion | flops 606928128 | bytes 5122048 | tf_op jit(solution)/shard_map/dot_general | solution.py:369
  142.9 1.3 multiply_convert_fusion.1
  144.2 0.8 exp.28
  145.6 2.7 %fusion.71 = f32[2,384,768]{2,1,0:T(8,128)S(1)} fusion(bf16[2,384,768]{2,1,0:T(8,128)(2,1)} %bitcast.175, bf16[768,768,1]{1,0,2:T(8,128)(2,1)} %bitcast.171), kind=kOutput, calls=%fused_computation.187 | convolution fusion | flops 905969664 | bytes 4718592 | tf_op jit(solution)/shard_map/dot_general | solution.py:374
  148.4 1.4 copy-done.8
  149.8 0.9 fusion.15.part
  150.6 23.9 %exchange_3.1 = (bf16[32,24,768]{2,1,0:T(8,128)(2,1)}, f32[32,8,128]{2,1,0:T(8,128)}, bf16[384,768]{1,0:T(8,128)(2,1)}) custom-call(bf16[32,24,768]{2,1,0:T(8,128)(2,1)} %bitcast.155, f32[32,8,128]{2,1,0:T(8,128)} %pad.55.es, bf16[384,768]{1,0:T(8,128)(2,1)} %fusion.15.part), custom_call_target="tpu_custom_call" | custom-call | tf_op jit(solution)/shard_map/exchange_3/pallas_call | solution.py:175
  174.5 0.9 slice_reduce_fusion.1
  176.1 2.5 fusion.16
  179.3 11.4 %exchange_4.1 = (f32[8,8,128]{2,1,0:T(8,128)}, f32[8,8,128]{2,1,0:T(8,128)}) custom-call(f32[8,128]{1,0:T(8,128)} %pad.56.tot), custom_call_target="tpu_custom_call" | custom-call | tf_op jit(solution)/shard_map/exchange_4/pallas_call | solution.py:175
  190.7 0.8 reduce_sum.206
  191.6 3.8 %fusion.5 = bf16[384,768]{1,0:T(8,128)(2,1)} fusion(bf16[768,768]{1,0:T(8,128)(2,1)} %bitcast.174, bf16[384,768]{1,0:T(8,128)(2,1)} %get-tuple-element.27, f32[2,384,768]{2,1,0:T(8,128)} %copy-done.8, s32[]{:T(128)S(6)} %select_n.302, f32[384]{0:T(512)S(1)} %fusion.53, f32[384]{0:T(512)} %fusion.55, s32[384]{0:T(512)} %eq.528, s32[384]{0:T(512)} %eq.524, ...), kind=kOutput, calls=%fused_computation.18 | convolution fusion | flops 459767808 | bytes 3554308 | tf_op jit(solution)/shard_map/dot_general | solution.py:387
  195.5 2.1 fusion.18
  197.6 1.4 reduce_sum.207
  199.0 1.3 slice.160
  200.2 1.3 reshape.511
  201.6 0.7 fusion.57
  204.1 50.6 %exchange_5.1 = (bf16[8,48,768]{2,1,0:T(8,128)(2,1)}, f32[32,8,128]{2,1,0:T(8,128)}, bf16[16,48,768]{2,1,0:T(8,128)(2,1)}, f32[8,128]{1,0:T(8,128)}) custom-call(bf16[8,48,768]{2,1,0:T(8,128)(2,1)} %bitcast.159, f32[32,8,128]{2,1,0:T(8,128)} %pad.58.inv, bf16[16,48,768]{2,1,0:T(8,128)(2,1)} %bitcast.157, f32[8,128]{1,0:T(8,128)} %pad.60.pw), custom_call_target="tpu_custom_call" | custom-call | tf_op jit(solution)/shard_map/exchange_5/pallas_call | solution.py:175
  254.7 1.8 convert_reduce_fusion.1
  256.5 1.3 slice_bitcast_fusion.8
  257.8 0.9 slice_reduce_fusion
  259.4 0.7 fusion.66
  260.1 3.1 %multiply_convert_fusion.2 = bf16[512,768]{1,0:T(8,128)(2,1)} fusion(bf16[768,768]{1,0:T(8,128)(2,1)} %bitcast.173, f32[768]{0:T(1024)S(1)} %fusion.66, s32[768]{0:T(1024)} %eq.532, s32[512]{0:T(512)} %iota_add_fusion), kind=kOutput, calls=%fused_computation.10 | convolution fusion | flops 606732288 | bytes 1974272 | tf_op jit(solution)/shard_map/dot_general | solution.py:419
  263.4 0.7 copy-done.4
  264.2 0.8 fusion.29
  (139 shorter events, 24.8 us)
Async XLA Ops:
  0.6 3.2 %copy-start = (bf16[2304,768]{1,0:T(8,128)(2,1)S(1)}, bf16[2304,768]{1,0:T(8,128)(2,1)}, u32[]{:S(2)}) copy-start(bf16[2304,768]{1,0:T(8,128)(2,1)} %param.9) | copy-start | bytes 10616836
  3.8 3.3 %copy-start.7 = (bf16[48,3072]{1,0:T(8,128)(2,1)S(1)}, bf16[48,3072]{1,0:T(8,128)(2,1)}, u32[]{:S(2)}) copy-start(bf16[48,3072]{1,0:T(8,128)(2,1)} %param.7) | copy-start | bytes 884740
  3.8 7.5 %copy-start.40 = (bf16[512,3072]{1,0:T(8,128)(2,1)S(1)}, bf16[512,3072]{1,0:T(8,128)(2,1)}, u32[]{:S(2)}) copy-start(bf16[512,3072]{1,0:T(8,128)(2,1)} %param.8) | copy-start | bytes 9437188
  5.8 0.7 copy-start.2
  7.2 4.2 %copy-start.1 = (bf16[3072,768]{1,0:T(8,128)(2,1)S(1)}, bf16[3072,768]{1,0:T(8,128)(2,1)}, u32[]{:S(2)}) copy-start(bf16[3072,768]{1,0:T(8,128)(2,1)} %param.10) | copy-start | bytes 14155780
  55.0 0.6 copy-start.9
  86.1 3.9 %copy-start.26 = (s32[384]{0:T(512)}, s32[384]{0:T(512)S(1)}, u32[]{:S(2)}) copy-start(s32[384]{0:T(512)S(1)} %eq.512) | copy-start | bytes 4612
  86.9 3.2 %copy-start.29 = (s32[384]{0:T(512)}, s32[384]{0:T(512)S(1)}, u32[]{:S(2)}) copy-start(s32[384]{0:T(512)S(1)} %eq.508) | copy-start | bytes 4612
  87.7 2.4 copy-start.32
  91.5 1.9 copy-start.16
  91.5 1.9 copy-start.18
  91.5 1.9 copy-start.20
  91.5 1.9 copy-start.22
  91.6 1.9 copy-start.24
  91.6 1.9 copy-start.27
  91.6 1.9 copy-start.30
  91.6 1.9 copy-start.33
  93.5 2.5 copy-start.6
  93.5 2.5 copy-start.41
  132.7 6.7 %copy-start.35 = (s32[768]{0:T(1024)S(1)}, s32[768]{0:T(1024)}, u32[]{:S(2)}) copy-start(s32[768]{0:T(1024)} %eq.532) | copy-start | bytes 9220
  132.7 6.6 %copy-start.38 = (s32[512]{0:T(512)S(1)}, s32[512]{0:T(512)}, u32[]{:S(2)}) copy-start(s32[512]{0:T(512)} %iota_add_fusion) | copy-start | bytes 6148
  142.3 0.6 copy-start.12
  142.9 1.3 copy-start.11
  148.3 1.4 copy-start.8
  176.1 15.3 %copy-start.14 = (f32[3,128]{1,0:T(4,128)S(1)}, f32[3,128]{1,0:T(4,128)}, u32[]{:S(2)}) copy-start(f32[3,128]{1,0:T(4,128)} %reshape_squeeze.10) | copy-start | bytes 4612
  176.1 15.4 %copy-start.15 = (f32[384]{0:T(512)S(1)}, f32[384]{0:T(512)}, u32[]{:S(2)}) copy-start(f32[384]{0:T(512)} %reshape_squeeze.9) | copy-start | bytes 4612
  176.1 15.4 %copy-start.17 = (s32[384]{0:T(512)S(1)}, s32[384]{0:T(512)}, u32[]{:S(2)}) copy-start(s32[384]{0:T(512)} %eq.500) | copy-start | bytes 4612
  191.5 3.9 %copy-start.13 = (s32[32,24]{1,0:T(8,128)S(1)}, s32[32,24]{1,0:T(8,128)}, u32[]{:S(2)}) copy-start(s32[32,24]{1,0:T(8,128)} %multiply_add_fusion) | copy-start | bytes 9220
  191.5 3.9 %copy-start.19 = (s32[384]{0:T(512)S(1)}, s32[384]{0:T(512)}, u32[]{:S(2)}) copy-start(s32[384]{0:T(512)} %eq.528) | copy-start | bytes 4612
  191.5 3.9 %copy-start.21 = (s32[384]{0:T(512)S(1)}, s32[384]{0:T(512)}, u32[]{:S(2)}) copy-start(s32[384]{0:T(512)} %eq.524) | copy-start | bytes 4612
  191.5 3.9 %copy-start.23 = (s32[384]{0:T(512)S(1)}, s32[384]{0:T(512)}, u32[]{:S(2)}) copy-start(s32[384]{0:T(512)} %eq.520) | copy-start | bytes 4612
  191.5 3.9 %copy-start.25 = (s32[384]{0:T(512)S(1)}, s32[384]{0:T(512)}, u32[]{:S(2)}) copy-start(s32[384]{0:T(512)} %eq.516) | copy-start | bytes 4612
  191.5 3.9 %copy-start.28 = (s32[384]{0:T(512)S(1)}, s32[384]{0:T(512)}, u32[]{:S(2)}) copy-start(s32[384]{0:T(512)} %copy-done.26) | copy-start | bytes 4612
  191.6 3.9 %copy-start.31 = (s32[384]{0:T(512)S(1)}, s32[384]{0:T(512)}, u32[]{:S(2)}) copy-start(s32[384]{0:T(512)} %copy-done.29) | copy-start | bytes 4612
  191.6 3.9 %copy-start.34 = (s32[384]{0:T(512)S(1)}, s32[384]{0:T(512)}, u32[]{:S(2)}) copy-start(s32[384]{0:T(512)} %copy-done.32) | copy-start | bytes 4612
  202.3 0.6 copy-start.36
  260.1 3.1 %copy-start.3 = (bf16[16,48,768]{2,1,0:T(8,128)(2,1)S(1)}, bf16[16,48,768]{2,1,0:T(8,128)(2,1)}, u32[]{:S(2)}) copy-start(bf16[16,48,768]{2,1,0:T(8,128)(2,1)} %get-tuple-element.35) | copy-start | bytes 3538948
  263.2 0.9 copy-start.4
  263.3 1.0 copy-start.5
  263.3 1.0 copy-start.10
  263.3 1.0 copy-start.37
  263.3 1.0 copy-start.39

commit v2 on v0

v2 whole, which is shorter than its diff:
```python
import jax
import jax.numpy as jnp
from jax import lax
from jax.experimental import pallas as pl
from jax.experimental.pallas import tpu as pltpu
from jax.sharding import PartitionSpec as P

logit_scale = 50.0
MESH = pl.DeviceIdType.MESH
F32 = jnp.float32
BF16 = jnp.bfloat16
I32 = jnp.int32
EMB = 768
CAP = 12
SLOTS = 2 * CAP
QB = 48
QD = 192
NN = (((1,), (0,)), ((), ()))
NT = (((1,), (1,)), ((), ()))
TN = (((0,), (0,)), ((), ()))


def mm(a, b, dims=NN):
    return lax.dot_general(a, b, dims, preferred_element_type=F32)


def rem(a, n):
    return lax.rem(a, n)


def quo(a, n):
    return lax.div(a, n)


def loop(lo, hi, body):
    def step(i, carry):
        body(i)
        return carry

    lax.fori_loop(lo, hi, step, 0)


def place():
    y = lax.axis_index("tower")
    dp = lax.axis_index("dp")
    return y, dp, quo(dp, 8), rem(quo(dp, 2), 4), rem(dp, 2)


class Route:
    def __init__(self, count, dest, source, slot, own, item=None):
        self.count, self.dest, self.source = count, dest, source
        self.slot, self.own, self.item = slot, own, item


def make_routes():
    y, dp, z, x, c = place()
    line = x * 2 + c
    turn = rem(y + 8 - z, 4)
    lead = quo(z, 4) * 4 + y
    at_home = rem(2 * z, 4) == y

    def plane_core(i):
        n = rem(y * 4 + x + i, 16)
        return quo(n, 4), z * 8 + rem(n, 4) * 2 + c

    def zcore(i):
        g = rem(z * 2 + c + i, 16)
        zz = quo(g, 2)
        return rem(turn + zz, 4), zz * 8 + x * 2 + rem(g, 2)

    def zline(i):
        zz = rem(z + i, 8)
        return rem(turn + zz, 4), zz * 8 + line

    def holder(i):
        zz = rem(z + i, 8)
        return rem(z + zz, 4), zz * 8 + line

    def home(i):
        k = rem(lead + i, 8)
        return rem(k, 4), (turn + 4 * quo(k, 4)) * 8 + line

    to_query = (rem(dp, 4), y * 16 + quo(dp, 4))
    to_passage = (quo(dp, 16), rem(dp, 16) * 4 + y)
    query_own = (to_query[0] == y) & (to_query[1] == dp)
    passage_own = (to_passage[0] == y) & (to_passage[1] == dp)
    return {
        "plane_core": Route(16, plane_core, plane_core, y * 4 + x, True, lambda i: rem(y * 4 + x + i, 16)),
        "zline": Route(8, zline, zline, z, True),
        "zcore": Route(16, zcore, zcore, z * 2 + c, True),
        "holder": Route(8, holder, home, lead, at_home),
        "home": Route(8, home, holder, z, at_home, lambda i: rem(lead + i, 8)),
        "to_query": Route(1, lambda i: to_query, lambda i: to_passage, 0, query_own),
        "to_passage": Route(1, lambda i: to_passage, lambda i: to_query, 0, passage_own),
    }


def each(route, far, near):
    if route.own is True:
        near()
    else:

        @pl.when(route.own)
        def _():
            near()

        @pl.when(jnp.logical_not(route.own))
        def _():
            far(0)

    if route.count > 1:
        loop(1, route.count, far)


class Transfer:
    def __init__(self, route, src, dst, sems):
        self.route, self.src, self.dst = route, src, dst
        self.send_sem, self.recv_sem = sems

    def copy(self, i):
        slot = self.route.slot
        return pltpu.make_async_remote_copy(
            src_ref=self.src(i),
            dst_ref=self.dst(slot),
            send_sem=self.send_sem.at[i],
            recv_sem=self.recv_sem.at[slot],
            device_id=self.route.dest(i),
            device_id_type=MESH,
        )

    def local(self):
        slot = self.route.slot
        return pltpu.make_async_copy(self.src(0), self.dst(slot), self.recv_sem.at[slot])

    def start(self):
        each(self.route, lambda i: self.copy(i).start(), lambda: self.local().start())

    def wait_slot(self, k):
        pltpu.make_async_copy(self.dst(k), self.dst(k), self.recv_sem.at[k]).wait()

    def wait_recv(self):
        loop(0, self.route.count, self.wait_slot)

    def wait_send(self):
        each(self.route, lambda i: self.copy(i).wait_send(), lambda: None)


class PlaneTransfer:
    def __init__(self, src, dst, sems):
        self.src, self.dst = src, dst
        self.send_sem, self.recv_sem = sems
        y, dp, z, x, c = place()
        self.base, self.line, self.me = z * 8, x * 2 + c, y * 8 + x * 2 + c

    def copy(self, row, spot):
        m = row * 8 + spot
        return pltpu.make_async_remote_copy(
            src_ref=self.src.at[m],
            dst_ref=self.dst.at[self.me],
            send_sem=self.send_sem.at[m],
            recv_sem=self.recv_sem.at[self.me],
            device_id=(row, self.base + spot),
            device_id_type=MESH,
        )

    def start_row(self, row):
        def go(t):
            spot = rem(self.line + t, 8)
            own = row * 8 + spot == self.me

            @pl.when(own)
            def _():
                pltpu.make_async_copy(
                    self.src.at[self.me], self.dst.at[self.me], self.recv_sem.at[self.me]
                ).start()

            @pl.when(jnp.logical_not(own))
            def _():
                self.copy(row, spot).start()

        loop(0, 8, go)

    def wait_row(self, row):
        def take(t):
            m = row * 8 + t
            pltpu.make_async_copy(self.dst.at[m], self.dst.at[m], self.recv_sem.at[m]).wait()

        loop(0, 8, take)

    def wait_send(self):
        def done(m):
            @pl.when(m != self.me)
            def _():
                self.copy(quo(m, 8), rem(m, 8)).wait_send()

        loop(0, 32, done)


def lane_of(shape):
    return lax.broadcasted_iota(I32, shape, len(shape) - 1)


def pack(column, base=0):
    groups = column.shape[0] // 8
    lane = lane_of((8, 128)) - base
    tile = jnp.zeros((8, 128), F32)
    for g in range(groups):
        tile = jnp.where(lane == g, column[8 * g : 8 * g + 8], tile)
    return tile


def unpack(tile, groups, base=0):
    lane = lane_of((8, 128)) - base
    parts = [jnp.sum(jnp.where(lane == g, tile, 0.0), axis=1, keepdims=True) for g in range(groups)]
    return jnp.concatenate(parts, axis=0)


def pack_slots(column):
    split = column.reshape(8, 3, 8, 1)
    lane = lane_of((8, 8, 128))
    tile = jnp.zeros((8, 8, 128), F32)
    for g in range(3):
        tile = jnp.where(lane == g, split[:, g], tile)
    return tile


def unpack_slots(tile):
    lane = lane_of((8, 8, 128))
    parts = [jnp.sum(jnp.where(lane == g, tile, 0.0), axis=2, keepdims=True)[:, None] for g in range(3)]
    return jnp.concatenate(parts, axis=1).reshape(QD, 1)


def three_parts(column):
    high = column.astype(BF16).astype(F32)
    rest = column - high
    middle = rest.astype(BF16).astype(F32)
    low = rest - middle
    lane = lane_of((column.shape[0], 128))
    parts = jnp.where(lane == 0, high, jnp.where(lane == 1, middle, jnp.where(lane == 2, low, 0.0)))
    return parts.astype(BF16)


def unit(projected):
    length = jnp.sqrt(jnp.sum(projected * projected, axis=1, keepdims=True) + 1e-06)
    return (projected / length).astype(BF16)


def flat(block):
    return block.astype(F32).reshape(block.shape[0] * block.shape[1], EMB)


SCRATCH = dict(
    wq=((2304, EMB), BF16),
    wp=((3072, EMB), BF16),
    hq=((QB, 2304), BF16),
    hp=((QB, 3072), BF16),
    hpool=((512, 3072), BF16),
    q48=((QB, EMB), BF16),
    p48=((QB, EMB), BF16),
    pool=((512, EMB), BF16),
    ids=((8, 256), I32),
    idh=((8, 8, 256), I32),
    qh=((2, 8, QB, EMB), BF16),
    ph=((16, QB, EMB), BF16),
    pp=((QB, EMB), BF16),
    qq=((QB, EMB), BF16),
    pick=((2, 768, QD), BF16),
    xs=((32, SLOTS, EMB), BF16),
    xr=((32, SLOTS, EMB), BF16),
    rs=((32, 8, 128), F32),
    rr=((32, 8, 128), F32),
    e=((768, 768), BF16),
    sums=((8, 128), F32),
    sumr=((16, 8, 128), F32),
    pos=((8, 128), F32),
    posr=((8, 8, 128), F32),
    nq=((768, EMB), F32),
    ns=((384, EMB), BF16),
    nr=((384, EMB), BF16),
    qn=((768, EMB), BF16),
    gs=((768, EMB), BF16),
    gr=((16, QB, EMB), BF16),
    chosen=((768, 512), BF16),
    ys=((32, SLOTS, EMB), BF16),
    yr=((32, SLOTS, EMB), BF16),
    es=((32, 8, 128), F32),
    er=((32, 8, 128), F32),
    tot=((8, 128), F32),
    totl=((8, 8, 128), F32),
    toth=((8, 8, 128), F32),
    invs=((32, 8, 128), F32),
    invr=((32, 8, 128), F32),
    hard=((2, QD, EMB), F32),
    zs=((8, QB, EMB), BF16),
    zr=((8, QB, EMB), BF16),
    pws=((8, 128), F32),
    pwr=((8, 128), F32),
    xw=((768, EMB), BF16),
)
PAIRS = dict(
    ids=8, q=8, p=16, pp=1, qq=1, fwd=8, x=32, r=32, sums=16, pos=8, n=1, y=32, e=32, totl=8, toth=8, inv=32, z=8,
    g=16, pw=1,
)


class Bag:
    pass


def step_kernel(wq, wp, hq, hp, hpool, ids, oq, op, on, *refs):
    v = Bag()
    for name, ref in zip(SCRATCH, refs):
        setattr(v, name, ref)
    rest = refs[len(SCRATCH) :]
    s = {name: (rest[2 * i], rest[2 * i + 1]) for i, name in enumerate(PAIRS)}
    in_sem = rest[2 * len(PAIRS)]
    routes = make_routes()
    y, dp, z, x, c = place()
    line = x * 2 + c
    turn = rem(y + 8 - z, 4)
    lead = quo(z, 4) * 4 + y

    inputs = [
        (ids, v.ids),
        (hq.at[pl.ds(pl.multiple_of(y * QB, QB), QB)], v.hq),
        (wq, v.wq),
        (hp, v.hp),
        (wp, v.wp),
        (hpool, v.hpool),
    ]
    loads = [pltpu.make_async_copy(a, b, in_sem.at[i]) for i, (a, b) in enumerate(inputs)]
    for load in loads:
        load.start()

    barrier = pltpu.get_barrier_semaphore()

    def greet(ty, td):
        pl.semaphore_signal(barrier, inc=1, device_id=(ty, td), device_id_type=MESH)

    wanted = 0
    for name in ("holder", "home", "to_query", "to_passage", "zcore"):
        route = routes[name]
        each(route, lambda i, route=route: greet(*route.source(i)), lambda: None)
        wanted = wanted + route.count - 1
        if route.own is not True:
            wanted = wanted + jnp.where(route.own, 0, 1)

    def greet_plane(i):
        m = rem(y * 8 + line + i, 32)
        greet(quo(m, 8), z * 8 + rem(m, 8))

    loop(1, 32, greet_plane)
    wanted = wanted + 31

    for i in (0, 1, 2):
        loads[i].wait()
    v.q48[...] = unit(mm(v.hq[...], v.wq[...]))
    pl.semaphore_wait(barrier, wanted)
    t_ids = Transfer(routes["holder"], lambda i: v.ids, lambda k: v.idh.at[k], s["ids"])
    t_q = Transfer(routes["holder"], lambda i: v.q48, lambda k: v.qh.at[c, k], s["q"])
    t_qq = Transfer(routes["to_passage"], lambda i: v.q48, lambda k: v.qq, s["qq"])
    t_ids.start()
    t_q.start()
    t_qq.start()
    for i in (3, 4):
        loads[i].wait()
    v.p48[...] = unit(mm(v.hp[...], v.wp[...]))
    t_p = Transfer(routes["plane_core"], lambda i: v.p48, lambda k: v.ph.at[k], s["p"])
    t_pp = Transfer(routes["to_query"], lambda i: v.p48, lambda k: v.pp, s["pp"])
    t_pp.start()
    t_p.start()
    loads[5].wait()

    def project_pool(i):
        part = pl.ds(pl.multiple_of(i * 256, 256), 256)
        v.pool[part, :] = unit(mm(v.hpool[part, :], v.wp[...]))

    loop(0, 2, project_pool)

    t_ids.wait_recv()
    before = (lax.broadcasted_iota(I32, (QD, QD), 0) < lane_of((QD, QD))).astype(F32).astype(BF16)
    member_row = lax.broadcasted_iota(I32, (32, QD), 0)
    slots, codes = [], []
    for half in range(2):
        held = v.idh[4 * half][:, :QD]
        owner = lax.shift_right_logical(held, 9)
        inside = (lax.shift_right_logical(owner, 3) & 7) == z
        target = jnp.where(inside, lax.shift_right_logical(owner, 6) * 8 + (owner & 7), -1)
        code = ((held & 511) + 1).astype(F32)
        names = [(member_row == target[k : k + 1]).astype(F32) for k in range(8)]
        count = names[0]
        for k in range(1, 8):
            count = count + names[k]
        running = mm(count.astype(BF16), before)
        start = (target * SLOTS + half * CAP).astype(F32)
        rows = []
        for k in range(8):
            rank = jnp.sum(names[k] * running, axis=0, keepdims=True)
            rows.append(jnp.where(target[k : k + 1] >= 0, start[k : k + 1] + rank, -1.0))
            running = running + names[k]
        slots.append(rows)
        codes.append([code[k : k + 1] for k in range(8)])

    def forward(k):
        return pltpu.make_async_remote_copy(
            src_ref=v.qh.at[c, k],
            dst_ref=v.qh.at[c, k],
            send_sem=s["fwd"][0].at[k],
            recv_sem=s["fwd"][1].at[k],
            device_id=(y, dp + 1 - 2 * c),
            device_id_type=MESH,
        )

    def hand_on(k):
        t_q.wait_slot(k)
        forward(k).start()

    loop(0, 8, hand_on)

    t_x = PlaneTransfer(v.xs, v.xr, s["x"])
    t_r = PlaneTransfer(v.rs, v.rr, s["r"])

    def ask(j):
        row = rem(y + j, 4)
        here = pl.ds(pl.multiple_of(row * QD, QD), QD)
        spot = (lax.broadcasted_iota(I32, (QD, QD), 0) + row * QD).astype(F32)
        found = jnp.zeros((QD, QD), F32)
        asked = jnp.zeros((QD, EMB), F32)
        for half in range(2):
            hits = jnp.zeros((QD, QD), F32)
            for k in range(8):
                hits = jnp.where(spot == slots[half][k], codes[half][k], hits)
            found = found + hits
            picked = jnp.where(hits > 0.0, 1.0, 0.0).astype(BF16)
            v.pick[half, here, :] = picked
            asked = asked + mm(picked, v.qh[c, 4 * half : 4 * half + 4].reshape(QD, EMB))
        v.xs[pl.ds(row * 8, 8)] = asked.reshape(8, SLOTS, EMB).astype(BF16)
        v.rs[pl.ds(row * 8, 8)] = pack_slots(jnp.sum(found, axis=1, keepdims=True))
        t_r.start_row(row)
        t_x.start_row(row)

    loop(0, 4, ask)

    t_pp.wait_recv()
    pos_exp = jnp.exp(logit_scale * jnp.sum(v.q48[...].astype(F32) * v.pp[...].astype(F32), axis=1, keepdims=True))
    v.pos[...] = pack(pos_exp, lead * 6)
    t_pos = Transfer(routes["holder"], lambda i: v.pos, lambda k: v.posr.at[k], s["pos"])
    t_pos.start()

    t_p.wait_recv()

    def taken(k):
        pltpu.make_async_copy(v.qh.at[1 - c, k], v.qh.at[1 - c, k], s["fwd"][1].at[k]).wait()

    loop(0, 8, taken)

    def queries(j):
        return v.qh[quo(j, 2), pl.ds(rem(j, 2) * 4, 4)].reshape(QD, EMB)

    def score(j, tile):
        here = pl.ds(pl.multiple_of(j * QD, QD), QD)
        passages = v.ph[...].reshape(768, EMB)
        grown = jnp.exp(logit_scale * mm(queries(j), passages, NT))
        low = grown.astype(BF16)
        v.e[here, :] = low
        v.nq[here, :] = mm(low, passages)
        return tile + pack(jnp.sum(grown, axis=1, keepdims=True), j * 24)

    v.sums[...] = lax.fori_loop(0, 4, score, jnp.zeros((8, 128), F32))
    t_sums = Transfer(routes["zcore"], lambda i: v.sums, lambda k: v.sumr.at[k], s["sums"])
    t_sums.start()
    v.ns[...] = v.nq[pl.ds(pl.multiple_of((1 - c) * 384, 384), 384), :].astype(BF16)
    send_n = pltpu.make_async_remote_copy(
        src_ref=v.ns,
        dst_ref=v.nr,
        send_sem=s["n"][0].at[0],
        recv_sem=s["n"][1].at[0],
        device_id=(y, dp + 1 - 2 * c),
        device_id_type=MESH,
    )
    send_n.start()
    t_sums.wait_recv()
    inv_batch = 1.0 / jnp.where(lane_of((8, 128)) < 96, jnp.sum(v.sumr[...], axis=0), 1.0)

    def scale_queries(j):
        here = pl.ds(pl.multiple_of(j * QD, QD), QD)
        v.qn[here, :] = (queries(j).astype(F32) * unpack(inv_batch, 24, j * 24)).astype(BF16)

    loop(0, 4, scale_queries)
    for j in range(3):
        v.gs[256 * j : 256 * j + 256, :] = mm(v.e[:, 256 * j : 256 * j + 256], v.qn[...], TN).astype(BF16)

    t_y = PlaneTransfer(v.ys, v.yr, s["y"])
    t_e = PlaneTransfer(v.es, v.er, s["e"])

    def answer(j):
        row = rem(y + 4 - j, 4)
        here = pl.ds(pl.multiple_of(row * QD, QD), QD)
        t_r.wait_row(row)
        t_x.wait_row(row)
        code = unpack_slots(v.rr[pl.ds(row * 8, 8)])
        chosen = jnp.where(code == (lane_of((QD, 512)) + 1).astype(F32), 1.0, 0.0).astype(BF16)
        v.chosen[here, :] = chosen
        named = mm(chosen, v.pool[...])
        asked = flat(v.xr[pl.ds(row * 8, 8)])
        neg_exp = jnp.exp(logit_scale * jnp.sum(asked * named, axis=1, keepdims=True))
        v.es[pl.ds(row * 8, 8)] = pack_slots(neg_exp)
        t_e.start_row(row)
        v.ys[pl.ds(row * 8, 8)] = (neg_exp * named).reshape(8, SLOTS, EMB).astype(BF16)
        t_y.start_row(row)

    loop(0, 4, answer)

    def total(j, carry):
        row = rem(y + j, 4)
        here = pl.ds(pl.multiple_of(row * QD, QD), QD)
        t_e.wait_row(row)
        parts = three_parts(unpack_slots(v.er[pl.ds(row * 8, 8)]))
        return tuple(carry[half] + mm(v.pick[half, here, :], parts, TN) for half in range(2))

    both = lax.fori_loop(0, 4, total, (jnp.zeros((QD, 128), F32), jnp.zeros((QD, 128), F32)))
    column = jnp.concatenate([jnp.sum(t, axis=1, keepdims=True) for t in both], axis=0)
    v.tot[...] = pack(column)
    t_totl = Transfer(routes["zline"], lambda i: v.tot, lambda k: v.totl.at[k], s["totl"])
    t_toth = Transfer(routes["home"], lambda i: v.tot, lambda k: v.toth.at[k], s["toth"])
    t_totl.start()
    t_toth.start()
    t_pos.wait_recv()
    t_totl.wait_recv()
    hard_total = jnp.sum(v.totl[...], axis=0) + jnp.sum(v.posr[...], axis=0)
    inv_hard_tile = 1.0 / jnp.where(lane_of((8, 128)) < 48, hard_total, 1.0)
    inv_hard = [unpack(inv_hard_tile, 24, 24 * half) for half in range(2)]
    inv_parts = [three_parts(inv_hard[half]) for half in range(2)]
    t_inv = PlaneTransfer(v.invs, v.invr, s["inv"])

    def tell(j):
        row = rem(y + j, 4)
        here = pl.ds(pl.multiple_of(row * QD, QD), QD)
        shares = mm(v.pick[0, here, :], inv_parts[0]) + mm(v.pick[1, here, :], inv_parts[1])
        v.invs[pl.ds(row * 8, 8)] = pack_slots(jnp.sum(shares, axis=1, keepdims=True))
        t_inv.start_row(row)

    loop(0, 4, tell)
    t_toth.wait_recv()
    own_total = unpack(jnp.sum(v.toth[...], axis=0), 6, lead * 6)
    pos_coef = pos_exp / (pos_exp + own_total) - 2.0
    v.pws[...] = pack(pos_coef)
    t_pw = Transfer(routes["to_passage"], lambda i: v.pws, lambda k: v.pwr, s["pw"])
    t_pw.start()

    v.hard[...] = jnp.zeros((2, QD, EMB), F32)

    def collect(j):
        row = rem(y + j, 4)
        here = pl.ds(pl.multiple_of(row * QD, QD), QD)
        t_y.wait_row(row)
        rows = flat(v.yr[pl.ds(row * 8, 8)]).astype(BF16)
        for half in range(2):
            v.hard[half] += mm(v.pick[half, here, :], rows, TN)

    loop(0, 4, collect)
    pltpu.make_async_copy(v.nr, v.nr, s["n"][1].at[0]).wait()
    t_z = Transfer(routes["home"], lambda i: v.zs.at[routes["home"].item(i)], lambda k: v.zr.at[k], s["z"])
    for half in range(2):
        mine = v.nq[pl.ds(pl.multiple_of(c * 384 + half * QD, QD), QD), :] + v.nr[half * QD : half * QD + QD, :].astype(F32)
        inv_own = unpack(inv_batch, 24, c * 48 + half * 24)
        mixed = mine * inv_own + v.hard[half] * inv_hard[half]
        v.zs[4 * half : 4 * half + 4] = mixed.astype(BF16).reshape(4, QB, EMB)
    t_z.start()
    core = routes["plane_core"]
    t_g = Transfer(
        core,
        lambda i: v.gs.at[pl.ds(pl.multiple_of(core.item(i) * QB, QB), QB), :],
        lambda k: v.gr.at[k],
        s["g"],
    )
    t_g.start()

    def weigh(j):
        row = rem(y + 4 - j, 4)
        here = pl.ds(pl.multiple_of(row * QD, QD), QD)
        t_inv.wait_row(row)
        share = unpack_slots(v.es[pl.ds(row * 8, 8)]) * unpack_slots(v.invr[pl.ds(row * 8, 8)])
        v.xw[here, :] = (flat(v.xr[pl.ds(row * 8, 8)]) * share).astype(BF16)

    loop(0, 4, weigh)
    for j in range(2):
        part = mm(v.chosen[:, 256 * j : 256 * j + 256], v.xw[...], TN)
        on[256 * j : 256 * j + 256, :] = (logit_scale * part).astype(BF16)

    t_z.wait_recv()
    summed = jnp.sum(v.zr[...].astype(F32), axis=0)
    oq[...] = (logit_scale * (summed + pos_coef * v.pp[...].astype(F32))).astype(BF16)
    t_pw.wait_recv()
    t_qq.wait_recv()
    t_g.wait_recv()
    summed = jnp.sum(v.gr[...].astype(F32), axis=0)
    coef = unpack(v.pwr[...], 6)
    op[...] = (logit_scale * (summed + coef * v.qq[...].astype(F32))).astype(BF16)

    for t in (t_ids, t_q, t_qq, t_pp, t_p, t_r, t_x, t_pos, t_sums, t_e, t_y, t_totl, t_toth, t_inv, t_pw, t_z, t_g):
        t.wait_send()
    loop(0, 8, lambda k: forward(k).wait_send())
    send_n.wait_send()


def shards(query_hidden, passage_hidden, pool_hidden, query_proj, passage_proj, negative_ids):
    ids = jnp.pad(negative_ids.T, ((0, 0), (0, 64)))
    scratch = [pltpu.VMEM(shape, dtype) for shape, dtype in SCRATCH.values()]
    for n in PAIRS.values():
        scratch += [pltpu.SemaphoreType.DMA((n,)), pltpu.SemaphoreType.DMA((n,))]
    scratch.append(pltpu.SemaphoreType.DMA((6,)))
    return pl.pallas_call(
        step_kernel,
        out_shape=[jax.ShapeDtypeStruct((n, EMB), BF16) for n in (QB, QB, 512)],
        in_specs=[pl.BlockSpec(memory_space=pl.ANY)] * 6,
        out_specs=[pl.BlockSpec(memory_space=pltpu.VMEM)] * 3,
        scratch_shapes=scratch,
        compiler_params=pltpu.CompilerParams(
            collective_id=1, has_side_effects=True, vmem_limit_bytes=60 * 1024 * 1024
        ),
        name="contrastive_step",
    )(query_proj, passage_proj, query_hidden, passage_hidden, pool_hidden, ids)


def solution(mesh):
    placed = (
        P("dp", None),
        P(("tower", "dp"), None),
        P(("tower", "dp"), None),
        P(),
        P(),
        P("dp", None),
    )
    return jax.shard_map(
        shards,
        mesh=mesh,
        in_specs=placed,
        out_specs=(P(("dp", "tower"), None), P(("tower", "dp"), None), P(("tower", "dp"), None)),
        check_vma=False,
    )
```

time: 397 us -> 128 us (0.32); the launches traced: 391 us -> 126 us
  waiting for transfers between devices: 157 us -> 0 us
  Pallas kernels: 0 us -> 119 us
  other arithmetic: 82.6 us -> 0 us
  local copies, waits for them, and re-layouts: 66.1 us -> 6.41 us
  matrix products: 36.8 us -> 0 us
  starting transfers between devices: 26.4 us -> 0 us
  between operations: 14 us -> 0.64 us
  blocking collectives: 8.14 us -> 0 us
    pallas_call x0 -> x1, Pallas kernels: none -> 119 us  [shards(): pl.pallas_call(step_kernel, out_shape=[jax.ShapeDtypeStruct((n, EMB), BF1...]
    reduce_scatter x2 -> x0, waiting for transfers between devices: 90.8 us -> none  [the longest x1 69.6 us: shards(): lax.psum_scatter(logit_scale * (product + extra_rows), 'dp', scatter_dime...]
    all_to_all x3 -> x0, waiting for transfers between devices: 65.9 us -> none  [the longest x1 35.3 us: shards(): lax.all_to_all(pool_unit[asked_ids], 'dp', split_axis=0, concat_axis=0, t...]
    dot_general x8 -> x0, matrix products: 36.8 us -> none  [the longest x3 11.7 us: unit_rows(): projected = jnp.dot(hidden, weight, preferred_element_type=jnp.float32)]
    another operation x3 -> x0, other arithmetic: 36.4 us -> none
    gather x4 -> x0, local copies, waits for them, and re-layouts: 33.6 us -> none  [the longest x1 17.1 us: shards(): pos_rows_coef[jnp.clip(offsets, 0, query_count - 1)]]
    all_to_all x3 -> x0, starting transfers between devices: 25.9 us -> none  [the longest x1 12.2 us: shards(): lax.all_to_all(requests, 'dp', split_axis=0, concat_axis=0, tiled=True)]
    scatter-add x2 -> x0, other arithmetic: 22.3 us -> none  [the longest x1 13.1 us: shards(): slot_grad = jnp.zeros((slot_total, emb_width), jnp.float32).at[position]....]
  transfers between devices with their start and end apart: 6 -> 0, of which waited for: 5 -> 0; matrix products, arithmetic and copies ran while one was open for 37% -> 0% of each run, Pallas kernels for 0% -> 0%
where the time goes in v2:
time: 128 us; the launch traced here: 126 us
  Pallas kernels  119 us (93%)
  local copies, waits for them, and re-layouts  6.41 us (5%)
    pallas_call x1, Pallas kernels, shards(): pl.pallas_call(step_kernel, out_shape=[jax.ShapeDtypeStruct((n, EMB), BF1...  119 us
    unnamed x3, local copies, waits for them, and re-layouts  5.1 us

profile of v2, /device:TPU:24, one launch (start us, length us, event | category | flops | bytes accessed | tf_op | source)
XLA Modules:
  0.0 126.0 jit_solution(13782395572196208140)
XLA Ops:
  0.6 1.3 %pad.4.ids = s32[8,256]{1,0:T(8,128)} pad(s32[8,192]{1,0:T(8,128)} %bitcast.1, s32[]{:T(128)} %constant.0.clone.1), padding=0_0x0_64 | pad | bytes 14340 | tf_op jit(solution)/shard_map/jit(_pad)/pad | solution.py:608
  1.9 119.0 %contrastive_step.1 = (bf16[48,768]{1,0:T(8,128)(2,1)}, bf16[48,768]{1,0:T(8,128)(2,1)}, bf16[512,768]{1,0:T(8,128)(2,1)}) custom-call(bf16[2304,768]{1,0:T(8,128)(2,1)} %wq.1, bf16[3072,768]{1,0:T(8,128)(2,1)} %wp.1, bf16[192,2304]{1,0:T(8,128)(2,1)} %hq.1, bf16[48,3072]{1,0:T(8,128)(2,1)} %hp.1, bf16[512,3072]{1,0:T(8,128)(2,1)} %hpool.1, s32[8,256]{1,0:T(8,128)} %pad.4.ids), custom_call_target="tpu_custom_call" | custom-call | tf_op jit(solution)/shard_map/contrastive_step/pallas_call | solution.py:613
  120.9 1.5 %copy.12 = bf16[48,768]{1,0:T(8,128)(2,1)} copy(bf16[48,768]{1,0:T(8,128)(2,1)} %get-tuple-element.6) | data formatting | bytes 147456
  122.4 1.5 %copy.13 = bf16[48,768]{1,0:T(8,128)(2,1)} copy(bf16[48,768]{1,0:T(8,128)(2,1)} %get-tuple-element.7) | data formatting | bytes 147456
  124.0 2.1 %copy.14 = bf16[512,768]{1,0:T(8,128)(2,1)} copy(bf16[512,768]{1,0:T(8,128)(2,1)} %get-tuple-element.8) | data formatting | bytes 1572864

commit v3 on v2

--- a/solution.py
+++ b/solution.py
@@ -76,6 +76,9 @@
         zz = rem(z + i, 8)
         return rem(z + zz, 4), zz * 8 + line
 
+    def column(i):
+        return y, (turn + 4 * rem(quo(z, 4) + i, 2)) * 8 + line
+
     def home(i):
         k = rem(lead + i, 8)
         return rem(k, 4), (turn + 4 * quo(k, 4)) * 8 + line
@@ -88,6 +91,7 @@
         "plane_core": Route(16, plane_core, plane_core, y * 4 + x, True, lambda i: rem(y * 4 + x + i, 16)),
         "zline": Route(8, zline, zline, z, True),
         "zcore": Route(16, zcore, zcore, z * 2 + c, True),
+        "column": Route(2, column, column, quo(z, 4), at_home),
         "holder": Route(8, holder, home, lead, at_home),
         "home": Route(8, home, holder, z, at_home, lambda i: rem(lead + i, 8)),
         "to_query": Route(1, lambda i: to_query, lambda i: to_passage, 0, query_own),
@@ -252,15 +256,15 @@
 SCRATCH = dict(
     wq=((2304, EMB), BF16),
     wp=((3072, EMB), BF16),
-    hq=((QB, 2304), BF16),
+    hq=((QD, 2304), BF16),
     hp=((QB, 3072), BF16),
     hpool=((512, 3072), BF16),
-    q48=((QB, EMB), BF16),
+    q192=((QD, EMB), BF16),
     p48=((QB, EMB), BF16),
     pool=((512, EMB), BF16),
-    ids=((8, 256), I32),
-    idh=((8, 8, 256), I32),
-    qh=((2, 8, QB, EMB), BF16),
+    ids=((8, QD), I32),
+    idh=((2, 8, QD), I32),
+    qh=((2, 2, QD, EMB), BF16),
     ph=((16, QB, EMB), BF16),
     pp=((QB, EMB), BF16),
     qq=((QB, EMB), BF16),
@@ -298,7 +302,7 @@
     xw=((768, EMB), BF16),
 )
 PAIRS = dict(
-    ids=8, q=8, p=16, pp=1, qq=1, fwd=8, x=32, r=32, sums=16, pos=8, n=1, y=32, e=32, totl=8, toth=8, inv=32, z=8,
+    ids=2, q=2, p=16, pp=1, qq=1, fwd=2, x=32, r=32, sums=16, pos=8, n=1, y=32, e=32, totl=8, toth=8, inv=32, z=8,
     g=16, pw=1,
 )
 
@@ -320,17 +324,30 @@
     turn = rem(y + 8 - z, 4)
     lead = quo(z, 4) * 4 + y
 
-    inputs = [
-        (ids, v.ids),
-        (hq.at[pl.ds(pl.multiple_of(y * QB, QB), QB)], v.hq),
-        (wq, v.wq),
-        (hp, v.hp),
-        (wp, v.wp),
-        (hpool, v.hpool),
-    ]
-    loads = [pltpu.make_async_copy(a, b, in_sem.at[i]) for i, (a, b) in enumerate(inputs)]
-    for load in loads:
-        load.start()
+    loads = {}
+    at = 0
+    for name, ref, into, pieces in (
+        ("ids", ids, v.ids, 1),
+        ("hq", hq, v.hq, 2),
+        ("wq", wq, v.wq, 4),
+        ("hp", hp, v.hp, 1),
+        ("wp", wp, v.wp, 4),
+        ("hpool", hpool, v.hpool, 4),
+    ):
+        size = into.shape[0] // pieces
+        loads[name] = []
+        for k in range(pieces):
+            part = pl.ds(k * size, size)
+            loads[name].append(pltpu.make_async_copy(ref.at[part], into.at[part], in_sem.at[at]))
+            at += 1
+    for group in loads.values():
+        for load in group:
+            load.start()
+
+    def loaded(*names):
+        for name in names:
+            for load in loads[name]:
+                load.wait()
 
     barrier = pltpu.get_barrier_semaphore()
 
@@ -338,7 +355,7 @@
         pl.semaphore_signal(barrier, inc=1, device_id=(ty, td), device_id_type=MESH)
 
     wanted = 0
-    for name in ("holder", "home", "to_query", "to_passage", "zcore"):
+    for name in ("column", "holder", "home", "to_query", "to_passage", "zcore"):
         route = routes[name]
         each(route, lambda i, route=route: greet(*route.source(i)), lambda: None)
         wanted = wanted + route.count - 1
@@ -352,24 +369,23 @@
     loop(1, 32, greet_plane)
     wanted = wanted + 31
 
-    for i in (0, 1, 2):
-        loads[i].wait()
-    v.q48[...] = unit(mm(v.hq[...], v.wq[...]))
+    loaded("ids")
+    loaded("hq", "wq")
+    v.q192[...] = unit(mm(v.hq[...], v.wq[...]))
+    own_q = v.q192.at[pl.ds(pl.multiple_of(y * QB, QB), QB), :]
     pl.semaphore_wait(barrier, wanted)
-    t_ids = Transfer(routes["holder"], lambda i: v.ids, lambda k: v.idh.at[k], s["ids"])
-    t_q = Transfer(routes["holder"], lambda i: v.q48, lambda k: v.qh.at[c, k], s["q"])
-    t_qq = Transfer(routes["to_passage"], lambda i: v.q48, lambda k: v.qq, s["qq"])
+    t_ids = Transfer(routes["column"], lambda i: v.ids, lambda k: v.idh.at[k], s["ids"])
+    t_q = Transfer(routes["column"], lambda i: v.q192, lambda k: v.qh.at[c, k], s["q"])
+    t_qq = Transfer(routes["to_passage"], lambda i: own_q, lambda k: v.qq, s["qq"])
     t_ids.start()
     t_q.start()
-    t_qq.start()
-    for i in (3, 4):
-        loads[i].wait()
+    loaded("hp", "wp")
     v.p48[...] = unit(mm(v.hp[...], v.wp[...]))
     t_p = Transfer(routes["plane_core"], lambda i: v.p48, lambda k: v.ph.at[k], s["p"])
     t_pp = Transfer(routes["to_query"], lambda i: v.p48, lambda k: v.pp, s["pp"])
+    t_p.start()
     t_pp.start()
-    t_p.start()
-    loads[5].wait()
+    loaded("hpool")
 
     def project_pool(i):
         part = pl.ds(pl.multiple_of(i * 256, 256), 256)
@@ -382,7 +398,7 @@
     member_row = lax.broadcasted_iota(I32, (32, QD), 0)
     slots, codes = [], []
     for half in range(2):
-        held = v.idh[4 * half][:, :QD]
+        held = v.idh[half]
         owner = lax.shift_right_logical(held, 9)
         inside = (lax.shift_right_logical(owner, 3) & 7) == z
         target = jnp.where(inside, lax.shift_right_logical(owner, 6) * 8 + (owner & 7), -1)
@@ -415,7 +431,7 @@
         t_q.wait_slot(k)
         forward(k).start()
 
-    loop(0, 8, hand_on)
+    loop(0, 2, hand_on)
 
     t_x = PlaneTransfer(v.xs, v.xr, s["x"])
     t_r = PlaneTransfer(v.rs, v.rr, s["r"])
@@ -433,7 +449,7 @@
             found = found + hits
             picked = jnp.where(hits > 0.0, 1.0, 0.0).astype(BF16)
             v.pick[half, here, :] = picked
-            asked = asked + mm(picked, v.qh[c, 4 * half : 4 * half + 4].reshape(QD, EMB))
+            asked = asked + mm(picked, v.qh[c, half])
         v.xs[pl.ds(row * 8, 8)] = asked.reshape(8, SLOTS, EMB).astype(BF16)
         v.rs[pl.ds(row * 8, 8)] = pack_slots(jnp.sum(found, axis=1, keepdims=True))
         t_r.start_row(row)
@@ -442,7 +458,7 @@
     loop(0, 4, ask)
 
     t_pp.wait_recv()
-    pos_exp = jnp.exp(logit_scale * jnp.sum(v.q48[...].astype(F32) * v.pp[...].astype(F32), axis=1, keepdims=True))
+    pos_exp = jnp.exp(logit_scale * jnp.sum(own_q[...].astype(F32) * v.pp[...].astype(F32), axis=1, keepdims=True))
     v.pos[...] = pack(pos_exp, lead * 6)
     t_pos = Transfer(routes["holder"], lambda i: v.pos, lambda k: v.posr.at[k], s["pos"])
     t_pos.start()
@@ -452,10 +468,10 @@
     def taken(k):
         pltpu.make_async_copy(v.qh.at[1 - c, k], v.qh.at[1 - c, k], s["fwd"][1].at[k]).wait()
 
-    loop(0, 8, taken)
+    loop(0, 2, taken)
 
     def queries(j):
-        return v.qh[quo(j, 2), pl.ds(rem(j, 2) * 4, 4)].reshape(QD, EMB)
+        return v.qh[quo(j, 2), rem(j, 2)]
 
     def score(j, tile):
         here = pl.ds(pl.multiple_of(j * QD, QD), QD)
@@ -510,6 +526,7 @@
         t_y.start_row(row)
 
     loop(0, 4, answer)
+    t_qq.start()
 
     def total(j, carry):
         row = rem(y + j, 4)
@@ -525,6 +542,15 @@
     t_toth = Transfer(routes["home"], lambda i: v.tot, lambda k: v.toth.at[k], s["toth"])
     t_totl.start()
     t_toth.start()
+    t_y.wait_send()
+    core = routes["plane_core"]
+    t_g = Transfer(
+        core,
+        lambda i: v.gs.at[pl.ds(pl.multiple_of(core.item(i) * QB, QB), QB), :],
+        lambda k: v.gr.at[k],
+        s["g"],
+    )
+    t_g.start()
     t_pos.wait_recv()
     t_totl.wait_recv()
     hard_total = jnp.sum(v.totl[...], axis=0) + jnp.sum(v.posr[...], axis=0)
@@ -567,15 +593,6 @@
         mixed = mine * inv_own + v.hard[half] * inv_hard[half]
         v.zs[4 * half : 4 * half + 4] = mixed.astype(BF16).reshape(4, QB, EMB)
     t_z.start()
-    core = routes["plane_core"]
-    t_g = Transfer(
-        core,
-        lambda i: v.gs.at[pl.ds(pl.multiple_of(core.item(i) * QB, QB), QB), :],
-        lambda k: v.gr.at[k],
-        s["g"],
-    )
-    t_g.start()
-
     def weigh(j):
         row = rem(y + 4 - j, 4)
         here = pl.ds(pl.multiple_of(row * QD, QD), QD)
@@ -598,19 +615,24 @@
     coef = unpack(v.pwr[...], 6)
     op[...] = (logit_scale * (summed + coef * v.qq[...].astype(F32))).astype(BF16)
 
-    for t in (t_ids, t_q, t_qq, t_pp, t_p, t_r, t_x, t_pos, t_sums, t_e, t_y, t_totl, t_toth, t_inv, t_pw, t_z, t_g):
+    for t in (t_ids, t_q, t_qq, t_pp, t_p, t_r, t_x, t_pos, t_sums, t_e, t_totl, t_toth, t_inv, t_pw, t_z, t_g):
         t.wait_send()
-    loop(0, 8, lambda k: forward(k).wait_send())
+    loop(0, 2, lambda k: forward(k).wait_send())
     send_n.wait_send()
 
 
+def settle_kernel(q, p, n, oq, op, on):
+    oq[...] = q[...]
+    op[...] = p[...]
+    on[...] = n[...]
+
+
 def shards(query_hidden, passage_hidden, pool_hidden, query_proj, passage_proj, negative_ids):
-    ids = jnp.pad(negative_ids.T, ((0, 0), (0, 64)))
     scratch = [pltpu.VMEM(shape, dtype) for shape, dtype in SCRATCH.values()]
     for n in PAIRS.values():
         scratch += [pltpu.SemaphoreType.DMA((n,)), pltpu.SemaphoreType.DMA((n,))]
-    scratch.append(pltpu.SemaphoreType.DMA((6,)))
-    return pl.pallas_call(
+    scratch.append(pltpu.SemaphoreType.DMA((16,)))
+    results = pl.pallas_call(
         step_kernel,
         out_shape=[jax.ShapeDtypeStruct((n, EMB), BF16) for n in (QB, QB, 512)],
         in_specs=[pl.BlockSpec(memory_space=pl.ANY)] * 6,
@@ -620,7 +642,14 @@
             collective_id=1, has_side_effects=True, vmem_limit_bytes=60 * 1024 * 1024
         ),
         name="contrastive_step",
-    )(query_proj, passage_proj, query_hidden, passage_hidden, pool_hidden, ids)
+    )(query_proj, passage_proj, query_hidden, passage_hidden, pool_hidden, negative_ids.T)
+    return pl.pallas_call(
+        settle_kernel,
+        out_shape=[jax.ShapeDtypeStruct((n, EMB), BF16) for n in (QB, QB, 512)],
+        in_specs=[pl.BlockSpec(memory_space=pltpu.VMEM)] * 3,
+        out_specs=[pl.BlockSpec(memory_space=pltpu.VMEM)] * 3,
+        name="settle",
+    )(*results)
 
 
 def solution(mesh):

time: 128 us -> 115 us (0.90); the launches traced: 126 us -> 115 us
  local copies, waits for them, and re-layouts: 6.41 us -> 0 us
  Pallas kernels: 119 us -> 114 us
    pallas_call x1, Pallas kernels: 119 us -> 112 us  [shards(): pl.pallas_call(step_kernel, out_shape=[jax.ShapeDtypeStruct((n, EMB), BF1...]
    unnamed x3 -> x0, local copies, waits for them, and re-layouts: 5.1 us -> none
    pallas_call x0 -> x1, Pallas kernels: none -> 2.16 us  [shards(): pl.pallas_call(settle_kernel, out_shape=[jax.ShapeDtypeStruct((n, EMB), B...]
    pad x1 -> x0, local copies, waits for them, and re-layouts: 1.3 us -> none  [shards(): ids = jnp.pad(negative_ids.T, ((0, 0), (0, 64)))]
where the time goes in v3:
time: 115 us
  Pallas kernels  114 us (99%)
    pallas_call x1, Pallas kernels, shards(): pl.pallas_call(step_kernel, out_shape=[jax.ShapeDtypeStruct((n, EMB), BF1...  112 us

profile of v3, /device:TPU:24, one launch (start us, length us, event | category | flops | bytes accessed | tf_op | source)
XLA Modules:
  0.0 115.1 jit_solution(2832957967303417406)
XLA Ops:
  0.6 112.3 %contrastive_step.1 = (bf16[48,768]{1,0:T(8,128)(2,1)}, bf16[48,768]{1,0:T(8,128)(2,1)}, bf16[512,768]{1,0:T(8,128)(2,1)}) custom-call(bf16[2304,768]{1,0:T(8,128)(2,1)} %wq.1, bf16[3072,768]{1,0:T(8,128)(2,1)} %wp.1, bf16[192,2304]{1,0:T(8,128)(2,1)} %hq.1, bf16[48,3072]{1,0:T(8,128)(2,1)} %hp.1, bf16[512,3072]{1,0:T(8,128)(2,1)} %hpool.1, s32[8,192]{1,0:T(8,128)} %bitcast.1), custom_call_target="tpu_custom_call" | custom-call | tf_op jit(solution)/shard_map/contrastive_step/pallas_call | solution.py:635
  112.9 2.2 %settle.1 = (bf16[48,768]{1,0:T(8,128)(2,1)}, bf16[48,768]{1,0:T(8,128)(2,1)}, bf16[512,768]{1,0:T(8,128)(2,1)}) custom-call(bf16[48,768]{1,0:T(8,128)(2,1)} %get-tuple-element.6.q, bf16[48,768]{1,0:T(8,128)(2,1)} %get-tuple-element.7.p, bf16[512,768]{1,0:T(8,128)(2,1)} %get-tuple-element.8.n), custom_call_target="tpu_custom_call" | custom-call | tf_op jit(solution)/shard_map/settle/pallas_call | solution.py:646

commit v4 on v3

--- a/solution.py
+++ b/solution.py
@@ -117,87 +117,89 @@
 
 
 class Transfer:
-    def __init__(self, route, src, dst, sems):
-        self.route, self.src, self.dst = route, src, dst
-        self.send_sem, self.recv_sem = sems
+    def __init__(self, route, src, into, sems):
+        self.route, self.src, self.into = route, src, into
+        self.send_sem, self.recv_sem = sems[0].at[0], sems[1].at[0]
+
+    def spot(self):
+        return self.into if self.route.count == 1 else self.into.at[self.route.slot]
 
     def copy(self, i):
-        slot = self.route.slot
         return pltpu.make_async_remote_copy(
             src_ref=self.src(i),
-            dst_ref=self.dst(slot),
-            send_sem=self.send_sem.at[i],
-            recv_sem=self.recv_sem.at[slot],
+            dst_ref=self.spot(),
+            send_sem=self.send_sem,
+            recv_sem=self.recv_sem,
             device_id=self.route.dest(i),
             device_id_type=MESH,
         )
 
     def local(self):
-        slot = self.route.slot
-        return pltpu.make_async_copy(self.src(0), self.dst(slot), self.recv_sem.at[slot])
+        return pltpu.make_async_copy(self.src(0), self.spot(), self.recv_sem)
 
     def start(self):
         each(self.route, lambda i: self.copy(i).start(), lambda: self.local().start())
 
-    def wait_slot(self, k):
-        pltpu.make_async_copy(self.dst(k), self.dst(k), self.recv_sem.at[k]).wait()
-
     def wait_recv(self):
-        loop(0, self.route.count, self.wait_slot)
+        pltpu.make_async_copy(self.into, self.into, self.recv_sem).wait()
 
     def wait_send(self):
-        each(self.route, lambda i: self.copy(i).wait_send(), lambda: None)
+        def taken(n):
+            part = self.into if n == self.route.count else self.into.at[pl.ds(0, n)]
+            pltpu.make_async_copy(part, part, self.send_sem).wait()
+
+        n = self.route.count
+        if self.route.own is True:
+            taken(n - 1)
+        else:
+            if n > 1:
+
+                @pl.when(self.route.own)
+                def _():
+                    taken(n - 1)
+
+            @pl.when(jnp.logical_not(self.route.own))
+            def _():
+                taken(n)
 
 
 class PlaneTransfer:
-    def __init__(self, src, dst, sems):
-        self.src, self.dst = src, dst
-        self.send_sem, self.recv_sem = sems
+    def __init__(self, src, dst, sems, spots):
+        self.src, self.dst, self.spots = src, dst, spots
+        self.send_sem, self.recv_sem = sems[0].at[0], sems[1]
         y, dp, z, x, c = place()
-        self.base, self.line, self.me = z * 8, x * 2 + c, y * 8 + x * 2 + c
-
-    def copy(self, row, spot):
-        m = row * 8 + spot
-        return pltpu.make_async_remote_copy(
-            src_ref=self.src.at[m],
-            dst_ref=self.dst.at[self.me],
-            send_sem=self.send_sem.at[m],
-            recv_sem=self.recv_sem.at[self.me],
-            device_id=(row, self.base + spot),
-            device_id_type=MESH,
-        )
-
-    def start_row(self, row):
-        def go(t):
-            spot = rem(self.line + t, 8)
-            own = row * 8 + spot == self.me
-
-            @pl.when(own)
-            def _():
-                pltpu.make_async_copy(
-                    self.src.at[self.me], self.dst.at[self.me], self.recv_sem.at[self.me]
-                ).start()
-
-            @pl.when(jnp.logical_not(own))
-            def _():
-                self.copy(row, spot).start()
-
-        loop(0, 8, go)
+        self.y, self.base, self.me = y, z * 8, y * 8 + x * 2 + c
+
+    def start_row(self, row, first):
+        def far(spot):
+            pltpu.make_async_remote_copy(
+                src_ref=self.src.at[row * 8 + spot],
+                dst_ref=self.dst.at[self.me],
+                send_sem=self.send_sem,
+                recv_sem=self.recv_sem.at[self.y],
+                device_id=(row, self.base + spot),
+                device_id_type=MESH,
+            ).start()
+
+        def near():
+            pltpu.make_async_copy(self.src.at[self.me], self.dst.at[self.me], self.recv_sem.at[self.y]).start()
+
+        if isinstance(first, bool):
+            near() if first else far(self.spots[0])
+        else:
+            pl.when(first)(near)
+            pl.when(jnp.logical_not(first))(lambda: far(self.spots[0]))
+
+        for spot in self.spots[1:]:
+            far(spot)
 
     def wait_row(self, row):
-        def take(t):
-            m = row * 8 + t
-            pltpu.make_async_copy(self.dst.at[m], self.dst.at[m], self.recv_sem.at[m]).wait()
-
-        loop(0, 8, take)
+        part = self.dst.at[pl.ds(row * 8, 8)]
+        pltpu.make_async_copy(part, part, self.recv_sem.at[row]).wait()
 
     def wait_send(self):
-        def done(m):
-            @pl.when(m != self.me)
-            def _():
-                self.copy(quo(m, 8), rem(m, 8)).wait_send()
-
-        loop(0, 32, done)
+        part = self.src.at[pl.ds(0, 31)]
+        pltpu.make_async_copy(part, part, self.send_sem).wait()
 
 
 def lane_of(shape):
@@ -285,8 +287,8 @@
     gs=((768, EMB), BF16),
     gr=((16, QB, EMB), BF16),
     chosen=((768, 512), BF16),
-    ys=((32, SLOTS, EMB), BF16),
-    yr=((32, SLOTS, EMB), BF16),
+    ys=((2, 32, SLOTS, EMB // 2), BF16),
+    yr=((2, 32, SLOTS, EMB // 2), BF16),
     es=((32, 8, 128), F32),
     er=((32, 8, 128), F32),
     tot=((8, 128), F32),
@@ -295,15 +297,14 @@
     invs=((32, 8, 128), F32),
     invr=((32, 8, 128), F32),
     hard=((2, QD, EMB), F32),
-    zs=((8, QB, EMB), BF16),
-    zr=((8, QB, EMB), BF16),
+    zs=((2, 8, QB, EMB // 2), BF16),
+    zr=((2, 8, QB, EMB // 2), BF16),
     pws=((8, 128), F32),
     pwr=((8, 128), F32),
     xw=((768, EMB), BF16),
 )
 PAIRS = dict(
-    ids=2, q=2, p=16, pp=1, qq=1, fwd=2, x=32, r=32, sums=16, pos=8, n=1, y=32, e=32, totl=8, toth=8, inv=32, z=8,
-    g=16, pw=1,
+    ids=1, q=1, p=1, pp=1, qq=1, fwd=2, x=4, r=4, sums=1, pos=1, n=1, y=4, y1=4, e=4, totl=1, toth=1, inv=4, z=1, z1=1, g=1, pw=1
 )
 
 
@@ -340,9 +341,13 @@
             part = pl.ds(k * size, size)
             loads[name].append(pltpu.make_async_copy(ref.at[part], into.at[part], in_sem.at[at]))
             at += 1
-    for group in loads.values():
-        for load in group:
-            load.start()
+
+    def fetch(*names):
+        for name in names:
+            for load in loads[name]:
+                load.start()
+
+    fetch("ids", "hq", "wq")
 
     def loaded(*names):
         for name in names:
@@ -369,22 +374,22 @@
     loop(1, 32, greet_plane)
     wanted = wanted + 31
 
-    loaded("ids")
-    loaded("hq", "wq")
+    fetch("hp", "wp")
+    loaded("ids", "hq", "wq")
+    fetch("hpool")
     v.q192[...] = unit(mm(v.hq[...], v.wq[...]))
     own_q = v.q192.at[pl.ds(pl.multiple_of(y * QB, QB), QB), :]
     pl.semaphore_wait(barrier, wanted)
-    t_ids = Transfer(routes["column"], lambda i: v.ids, lambda k: v.idh.at[k], s["ids"])
-    t_q = Transfer(routes["column"], lambda i: v.q192, lambda k: v.qh.at[c, k], s["q"])
-    t_qq = Transfer(routes["to_passage"], lambda i: own_q, lambda k: v.qq, s["qq"])
+    t_ids = Transfer(routes["column"], lambda i: v.ids, v.idh, s["ids"])
+    t_q = Transfer(routes["column"], lambda i: v.q192, v.qh.at[c], s["q"])
+    t_qq = Transfer(routes["to_passage"], lambda i: own_q, v.qq, s["qq"])
     t_ids.start()
     t_q.start()
     loaded("hp", "wp")
     v.p48[...] = unit(mm(v.hp[...], v.wp[...]))
-    t_p = Transfer(routes["plane_core"], lambda i: v.p48, lambda k: v.ph.at[k], s["p"])
-    t_pp = Transfer(routes["to_query"], lambda i: v.p48, lambda k: v.pp, s["pp"])
+    t_p = Transfer(routes["plane_core"], lambda i: v.p48, v.ph, s["p"])
+    t_pp = Transfer(routes["to_query"], lambda i: v.p48, v.pp, s["pp"])
     t_p.start()
-    t_pp.start()
     loaded("hpool")
 
     def project_pool(i):
@@ -427,14 +432,13 @@
             device_id_type=MESH,
         )
 
-    def hand_on(k):
-        t_q.wait_slot(k)
-        forward(k).start()
-
-    loop(0, 2, hand_on)
-
-    t_x = PlaneTransfer(v.xs, v.xr, s["x"])
-    t_r = PlaneTransfer(v.rs, v.rr, s["r"])
+    t_q.wait_recv()
+    forward(0).start()
+    forward(1).start()
+
+    spots = [rem(line + t, 8) for t in range(8)]
+    t_x = PlaneTransfer(v.xs, v.xr, s["x"], spots)
+    t_r = PlaneTransfer(v.rs, v.rr, s["r"], spots)
 
     def ask(j):
         row = rem(y + j, 4)
@@ -452,23 +456,20 @@
             asked = asked + mm(picked, v.qh[c, half])
         v.xs[pl.ds(row * 8, 8)] = asked.reshape(8, SLOTS, EMB).astype(BF16)
         v.rs[pl.ds(row * 8, 8)] = pack_slots(jnp.sum(found, axis=1, keepdims=True))
-        t_r.start_row(row)
-        t_x.start_row(row)
+        t_r.start_row(row, j == 0)
+        t_x.start_row(row, j == 0)
 
     loop(0, 4, ask)
 
-    t_pp.wait_recv()
-    pos_exp = jnp.exp(logit_scale * jnp.sum(own_q[...].astype(F32) * v.pp[...].astype(F32), axis=1, keepdims=True))
-    v.pos[...] = pack(pos_exp, lead * 6)
-    t_pos = Transfer(routes["holder"], lambda i: v.pos, lambda k: v.posr.at[k], s["pos"])
-    t_pos.start()
+    t_pp.start()
 
     t_p.wait_recv()
 
     def taken(k):
         pltpu.make_async_copy(v.qh.at[1 - c, k], v.qh.at[1 - c, k], s["fwd"][1].at[k]).wait()
 
-    loop(0, 2, taken)
+    taken(0)
+    taken(1)
 
     def queries(j):
         return v.qh[quo(j, 2), rem(j, 2)]
@@ -483,7 +484,7 @@
         return tile + pack(jnp.sum(grown, axis=1, keepdims=True), j * 24)
 
     v.sums[...] = lax.fori_loop(0, 4, score, jnp.zeros((8, 128), F32))
-    t_sums = Transfer(routes["zcore"], lambda i: v.sums, lambda k: v.sumr.at[k], s["sums"])
+    t_sums = Transfer(routes["zcore"], lambda i: v.sums, v.sumr, s["sums"])
     t_sums.start()
     v.ns[...] = v.nq[pl.ds(pl.multiple_of((1 - c) * 384, 384), 384), :].astype(BF16)
     send_n = pltpu.make_async_remote_copy(
@@ -506,8 +507,8 @@
     for j in range(3):
         v.gs[256 * j : 256 * j + 256, :] = mm(v.e[:, 256 * j : 256 * j + 256], v.qn[...], TN).astype(BF16)
 
-    t_y = PlaneTransfer(v.ys, v.yr, s["y"])
-    t_e = PlaneTransfer(v.es, v.er, s["e"])
+    t_y = [PlaneTransfer(v.ys.at[h], v.yr.at[h], s[name], spots) for h, name in enumerate(("y", "y1"))]
+    t_e = PlaneTransfer(v.es, v.er, s["e"], spots)
 
     def answer(j):
         row = rem(y + 4 - j, 4)
@@ -521,12 +522,24 @@
         asked = flat(v.xr[pl.ds(row * 8, 8)])
         neg_exp = jnp.exp(logit_scale * jnp.sum(asked * named, axis=1, keepdims=True))
         v.es[pl.ds(row * 8, 8)] = pack_slots(neg_exp)
-        t_e.start_row(row)
-        v.ys[pl.ds(row * 8, 8)] = (neg_exp * named).reshape(8, SLOTS, EMB).astype(BF16)
-        t_y.start_row(row)
+        t_e.start_row(row, j == 0)
+        rows = (neg_exp * named).reshape(8, SLOTS, EMB).astype(BF16)
+        for h in range(2):
+            v.ys[h, pl.ds(row * 8, 8)] = rows[:, :, 384 * h : 384 * h + 384]
 
     loop(0, 4, answer)
     t_qq.start()
+
+    def give(h, j):
+        t_y[h].start_row(rem(y + 4 - j, 4), j == 0)
+
+    give(0, 0)
+
+    t_pp.wait_recv()
+    pos_exp = jnp.exp(logit_scale * jnp.sum(own_q[...].astype(F32) * v.pp[...].astype(F32), axis=1, keepdims=True))
+    v.pos[...] = pack(pos_exp, lead * 6)
+    t_pos = Transfer(routes["holder"], lambda i: v.pos, v.posr, s["pos"])
+    t_pos.start()
 
     def total(j, carry):
         row = rem(y + j, 4)
@@ -538,61 +551,75 @@
     both = lax.fori_loop(0, 4, total, (jnp.zeros((QD, 128), F32), jnp.zeros((QD, 128), F32)))
     column = jnp.concatenate([jnp.sum(t, axis=1, keepdims=True) for t in both], axis=0)
     v.tot[...] = pack(column)
-    t_totl = Transfer(routes["zline"], lambda i: v.tot, lambda k: v.totl.at[k], s["totl"])
-    t_toth = Transfer(routes["home"], lambda i: v.tot, lambda k: v.toth.at[k], s["toth"])
+    t_totl = Transfer(routes["zline"], lambda i: v.tot, v.totl, s["totl"])
+    t_toth = Transfer(routes["home"], lambda i: v.tot, v.toth, s["toth"])
     t_totl.start()
     t_toth.start()
-    t_y.wait_send()
-    core = routes["plane_core"]
-    t_g = Transfer(
-        core,
-        lambda i: v.gs.at[pl.ds(pl.multiple_of(core.item(i) * QB, QB), QB), :],
-        lambda k: v.gr.at[k],
-        s["g"],
-    )
-    t_g.start()
+    loop(1, 4, lambda j: give(0, j))
+    loop(0, 4, lambda j: give(1, j))
     t_pos.wait_recv()
     t_totl.wait_recv()
     hard_total = jnp.sum(v.totl[...], axis=0) + jnp.sum(v.posr[...], axis=0)
     inv_hard_tile = 1.0 / jnp.where(lane_of((8, 128)) < 48, hard_total, 1.0)
     inv_hard = [unpack(inv_hard_tile, 24, 24 * half) for half in range(2)]
     inv_parts = [three_parts(inv_hard[half]) for half in range(2)]
-    t_inv = PlaneTransfer(v.invs, v.invr, s["inv"])
+    t_inv = PlaneTransfer(v.invs, v.invr, s["inv"], spots)
 
     def tell(j):
         row = rem(y + j, 4)
         here = pl.ds(pl.multiple_of(row * QD, QD), QD)
         shares = mm(v.pick[0, here, :], inv_parts[0]) + mm(v.pick[1, here, :], inv_parts[1])
         v.invs[pl.ds(row * 8, 8)] = pack_slots(jnp.sum(shares, axis=1, keepdims=True))
-        t_inv.start_row(row)
+        t_inv.start_row(row, j == 0)
 
     loop(0, 4, tell)
     t_toth.wait_recv()
     own_total = unpack(jnp.sum(v.toth[...], axis=0), 6, lead * 6)
     pos_coef = pos_exp / (pos_exp + own_total) - 2.0
     v.pws[...] = pack(pos_coef)
-    t_pw = Transfer(routes["to_passage"], lambda i: v.pws, lambda k: v.pwr, s["pw"])
+    t_pw = Transfer(routes["to_passage"], lambda i: v.pws, v.pwr, s["pw"])
     t_pw.start()
 
     v.hard[...] = jnp.zeros((2, QD, EMB), F32)
 
-    def collect(j):
-        row = rem(y + j, 4)
-        here = pl.ds(pl.multiple_of(row * QD, QD), QD)
-        t_y.wait_row(row)
-        rows = flat(v.yr[pl.ds(row * 8, 8)]).astype(BF16)
+    def collect(h):
+        lanes = slice(384 * h, 384 * h + 384)
+
+        def gather(j):
+            row = rem(y + j, 4)
+            here = pl.ds(pl.multiple_of(row * QD, QD), QD)
+            t_y[h].wait_row(row)
+            rows = v.yr[h, pl.ds(row * 8, 8)].astype(F32).reshape(QD, 384).astype(BF16)
+            for half in range(2):
+                v.hard[half, :, lanes] += mm(v.pick[half, here, :], rows, TN)
+
+        loop(0, 4, gather)
         for half in range(2):
-            v.hard[half] += mm(v.pick[half, here, :], rows, TN)
-
-    loop(0, 4, collect)
+            own = v.nq[pl.ds(pl.multiple_of(c * 384 + half * QD, QD), QD), lanes]
+            mine = own + v.nr[half * QD : half * QD + QD, lanes].astype(F32)
+            inv_own = unpack(inv_batch, 24, c * 48 + half * 24)
+            mixed = mine * inv_own + v.hard[half, :, lanes] * inv_hard[half]
+            v.zs[h, 4 * half : 4 * half + 4] = mixed.astype(BF16).reshape(4, QB, 384)
+
+    home = routes["home"]
+    t_z = [
+        Transfer(home, lambda i, h=h: v.zs.at[h, home.item(i)], v.zr.at[h], s[name])
+        for h, name in enumerate(("z", "z1"))
+    ]
     pltpu.make_async_copy(v.nr, v.nr, s["n"][1].at[0]).wait()
-    t_z = Transfer(routes["home"], lambda i: v.zs.at[routes["home"].item(i)], lambda k: v.zr.at[k], s["z"])
-    for half in range(2):
-        mine = v.nq[pl.ds(pl.multiple_of(c * 384 + half * QD, QD), QD), :] + v.nr[half * QD : half * QD + QD, :].astype(F32)
-        inv_own = unpack(inv_batch, 24, c * 48 + half * 24)
-        mixed = mine * inv_own + v.hard[half] * inv_hard[half]
-        v.zs[4 * half : 4 * half + 4] = mixed.astype(BF16).reshape(4, QB, EMB)
-    t_z.start()
+    collect(0)
+    t_z[0].start()
+    core = routes["plane_core"]
+    t_g = Transfer(
+        core,
+        lambda i: v.gs.at[pl.ds(pl.multiple_of(core.item(i) * QB, QB), QB), :],
+        v.gr,
+        s["g"],
+    )
+    t_g.start()
+    collect(1)
+    t_z[1].start()
+
     def weigh(j):
         row = rem(y + 4 - j, 4)
         here = pl.ds(pl.multiple_of(row * QD, QD), QD)
@@ -605,9 +632,11 @@
         part = mm(v.chosen[:, 256 * j : 256 * j + 256], v.xw[...], TN)
         on[256 * j : 256 * j + 256, :] = (logit_scale * part).astype(BF16)
 
-    t_z.wait_recv()
-    summed = jnp.sum(v.zr[...].astype(F32), axis=0)
-    oq[...] = (logit_scale * (summed + pos_coef * v.pp[...].astype(F32))).astype(BF16)
+    for h in range(2):
+        t_z[h].wait_recv()
+        lanes = slice(384 * h, 384 * h + 384)
+        summed = jnp.sum(v.zr[h].astype(F32), axis=0)
+        oq[:, lanes] = (logit_scale * (summed + pos_coef * v.pp[:, lanes].astype(F32))).astype(BF16)
     t_pw.wait_recv()
     t_qq.wait_recv()
     t_g.wait_recv()
@@ -615,9 +644,10 @@
     coef = unpack(v.pwr[...], 6)
     op[...] = (logit_scale * (summed + coef * v.qq[...].astype(F32))).astype(BF16)
 
-    for t in (t_ids, t_q, t_qq, t_pp, t_p, t_r, t_x, t_pos, t_sums, t_e, t_totl, t_toth, t_inv, t_pw, t_z, t_g):
+    for t in (t_ids, t_q, t_qq, t_pp, t_p, t_r, t_x, t_pos, t_sums, t_e, *t_y, t_totl, t_toth, t_inv, t_pw, *t_z, t_g):
         t.wait_send()
-    loop(0, 2, lambda k: forward(k).wait_send())
+    forward(0).wait_send()
+    forward(1).wait_send()
     send_n.wait_send()
 
 

time: 115 us -> 106 us (0.922)
  Pallas kernels: 114 us -> 104 us
    pallas_call x1, Pallas kernels: 112 us -> 102 us  [shards(): pl.pallas_call(step_kernel, out_shape=[jax.ShapeDtypeStruct((n, EMB), BF1...]
where the time goes in v4:
time: 106 us; the launch traced here: 105 us
  Pallas kernels  104 us (98%)
    pallas_call x1, Pallas kernels, shards(): pl.pallas_call(step_kernel, out_shape=[jax.ShapeDtypeStruct((n, EMB), BF1...  102 us
    pallas_call x1, Pallas kernels, shards(): pl.pallas_call(settle_kernel, out_shape=[jax.ShapeDtypeStruct((n, EMB), B...  2.16 us

profile of v4, /device:TPU:24, one launch (start us, length us, event | category | flops | bytes accessed | tf_op | source)
XLA Modules:
  0.0 105.1 jit_solution(4306986418407444228)
XLA Ops:
  0.6 102.3 %contrastive_step.1 = (bf16[48,768]{1,0:T(8,128)(2,1)}, bf16[48,768]{1,0:T(8,128)(2,1)}, bf16[512,768]{1,0:T(8,128)(2,1)}) custom-call(bf16[2304,768]{1,0:T(8,128)(2,1)} %wq.1, bf16[3072,768]{1,0:T(8,128)(2,1)} %wp.1, bf16[192,2304]{1,0:T(8,128)(2,1)} %hq.1, bf16[48,3072]{1,0:T(8,128)(2,1)} %hp.1, bf16[512,3072]{1,0:T(8,128)(2,1)} %hpool.1, s32[8,192]{1,0:T(8,128)} %bitcast.1), custom_call_target="tpu_custom_call" | custom-call | tf_op jit(solution)/shard_map/contrastive_step/pallas_call | solution.py:665
  103.0 2.2 %settle.1 = (bf16[48,768]{1,0:T(8,128)(2,1)}, bf16[48,768]{1,0:T(8,128)(2,1)}, bf16[512,768]{1,0:T(8,128)(2,1)}) custom-call(bf16[48,768]{1,0:T(8,128)(2,1)} %get-tuple-element.6.q, bf16[48,768]{1,0:T(8,128)(2,1)} %get-tuple-element.7.p, bf16[512,768]{1,0:T(8,128)(2,1)} %get-tuple-element.8.n), custom_call_target="tpu_custom_call" | custom-call | tf_op jit(solution)/shard_map/settle/pallas_call | solution.py:676

commit v5 on v4

--- a/solution.py
+++ b/solution.py
@@ -60,8 +60,14 @@
     at_home = rem(2 * z, 4) == y
 
     def plane_core(i):
-        n = rem(y * 4 + x + i, 16)
-        return quo(n, 4), z * 8 + rem(n, 4) * 2 + c
+        n = rem(x * 4 + y + i, 16)
+        return rem(n, 4), z * 8 + quo(n, 4) * 2 + c
+
+    def xline(i):
+        return y, z * 8 + rem(x + i, 4) * 2 + c
+
+    def yline(i):
+        return rem(y + i, 4), dp
 
     def zcore(i):
         g = rem(z * 2 + c + i, 16)
@@ -88,7 +94,9 @@
     query_own = (to_query[0] == y) & (to_query[1] == dp)
     passage_own = (to_passage[0] == y) & (to_passage[1] == dp)
     return {
-        "plane_core": Route(16, plane_core, plane_core, y * 4 + x, True, lambda i: rem(y * 4 + x + i, 16)),
+        "plane_core": Route(16, plane_core, plane_core, x * 4 + y, True),
+        "xline": Route(4, xline, xline, x, True, lambda i: rem(x + i, 4)),
+        "yline": Route(4, yline, yline, y, True, lambda i: rem(y + i, 4)),
         "zline": Route(8, zline, zline, z, True),
         "zcore": Route(16, zcore, zcore, z * 2 + c, True),
         "column": Route(2, column, column, quo(z, 4), at_home),
@@ -285,7 +293,9 @@
     nr=((384, EMB), BF16),
     qn=((768, EMB), BF16),
     gs=((768, EMB), BF16),
-    gr=((16, QB, EMB), BF16),
+    gx=((4, QD, EMB), BF16),
+    gy=((QD, EMB), BF16),
+    gr=((4, QB, EMB), BF16),
     chosen=((768, 512), BF16),
     ys=((2, 32, SLOTS, EMB // 2), BF16),
     yr=((2, 32, SLOTS, EMB // 2), BF16),
@@ -304,7 +314,7 @@
     xw=((768, EMB), BF16),
 )
 PAIRS = dict(
-    ids=1, q=1, p=1, pp=1, qq=1, fwd=2, x=4, r=4, sums=1, pos=1, n=1, y=4, y1=4, e=4, totl=1, toth=1, inv=4, z=1, z1=1, g=1, pw=1
+    ids=1, q=1, p=1, pp=1, qq=1, fwd=2, x=4, r=4, sums=1, pos=1, n=1, y=4, y1=4, e=4, totl=1, toth=1, inv=4, z=1, z1=1, gx=1, g=1, pw=1
 )
 
 
@@ -557,6 +567,16 @@
     t_toth.start()
     loop(1, 4, lambda j: give(0, j))
     loop(0, 4, lambda j: give(1, j))
+
+    across = routes["xline"]
+    t_gx = Transfer(
+        across,
+        lambda i: v.gs.at[pl.ds(pl.multiple_of(across.item(i) * QD, QD), QD), :],
+        v.gx,
+        s["gx"],
+    )
+    t_gx.start()
+
     t_pos.wait_recv()
     t_totl.wait_recv()
     hard_total = jnp.sum(v.totl[...], axis=0) + jnp.sum(v.posr[...], axis=0)
@@ -609,16 +629,16 @@
     pltpu.make_async_copy(v.nr, v.nr, s["n"][1].at[0]).wait()
     collect(0)
     t_z[0].start()
-    core = routes["plane_core"]
+    collect(1)
+    t_z[1].start()
+
+    t_gx.wait_recv()
+    v.gy[...] = jnp.sum(v.gx[...].astype(F32), axis=0).astype(BF16)
+    along = routes["yline"]
     t_g = Transfer(
-        core,
-        lambda i: v.gs.at[pl.ds(pl.multiple_of(core.item(i) * QB, QB), QB), :],
-        v.gr,
-        s["g"],
+        along, lambda i: v.gy.at[pl.ds(pl.multiple_of(along.item(i) * QB, QB), QB), :], v.gr, s["g"]
     )
     t_g.start()
-    collect(1)
-    t_z[1].start()
 
     def weigh(j):
         row = rem(y + 4 - j, 4)
@@ -644,7 +664,7 @@
     coef = unpack(v.pwr[...], 6)
     op[...] = (logit_scale * (summed + coef * v.qq[...].astype(F32))).astype(BF16)
 
-    for t in (t_ids, t_q, t_qq, t_pp, t_p, t_r, t_x, t_pos, t_sums, t_e, *t_y, t_totl, t_toth, t_inv, t_pw, *t_z, t_g):
+    for t in (t_ids, t_q, t_qq, t_pp, t_p, t_r, t_x, t_pos, t_sums, t_e, *t_y, t_totl, t_toth, t_inv, t_pw, *t_z, t_gx, t_g):
         t.wait_send()
     forward(0).wait_send()
     forward(1).wait_send()

time: 106 us -> 98.5 us (0.929)
  Pallas kernels: 104 us -> 96 us
    pallas_call x1, Pallas kernels: 102 us -> 93.9 us  [shards(): pl.pallas_call(step_kernel, out_shape=[jax.ShapeDtypeStruct((n, EMB), BF1...]
where the time goes in v5:
time: 98.5 us; the launch traced here: 96.7 us
  Pallas kernels  96 us (97%)
    pallas_call x1, Pallas kernels, shards(): pl.pallas_call(step_kernel, out_shape=[jax.ShapeDtypeStruct((n, EMB), BF1...  93.9 us
    pallas_call x1, Pallas kernels, shards(): pl.pallas_call(settle_kernel, out_shape=[jax.ShapeDtypeStruct((n, EMB), B...  2.16 us

profile of v5, /device:TPU:24, one launch (start us, length us, event | category | flops | bytes accessed | tf_op | source)
XLA Modules:
  0.0 96.7 jit_solution(12700144907288291741)
XLA Ops:
  0.6 93.9 %contrastive_step.1 = (bf16[48,768]{1,0:T(8,128)(2,1)}, bf16[48,768]{1,0:T(8,128)(2,1)}, bf16[512,768]{1,0:T(8,128)(2,1)}) custom-call(bf16[2304,768]{1,0:T(8,128)(2,1)} %wq.1, bf16[3072,768]{1,0:T(8,128)(2,1)} %wp.1, bf16[192,2304]{1,0:T(8,128)(2,1)} %hq.1, bf16[48,3072]{1,0:T(8,128)(2,1)} %hp.1, bf16[512,3072]{1,0:T(8,128)(2,1)} %hpool.1, s32[8,192]{1,0:T(8,128)} %bitcast.1), custom_call_target="tpu_custom_call" | custom-call | tf_op jit(solution)/shard_map/contrastive_step/pallas_call | solution.py:685
  94.5 2.2 %settle.1 = (bf16[48,768]{1,0:T(8,128)(2,1)}, bf16[48,768]{1,0:T(8,128)(2,1)}, bf16[512,768]{1,0:T(8,128)(2,1)}) custom-call(bf16[48,768]{1,0:T(8,128)(2,1)} %get-tuple-element.6.q, bf16[48,768]{1,0:T(8,128)(2,1)} %get-tuple-element.7.p, bf16[512,768]{1,0:T(8,128)(2,1)} %get-tuple-element.8.n), custom_call_target="tpu_custom_call" | custom-call | tf_op jit(solution)/shard_map/settle/pallas_call | solution.py:696

commit v6 on v5

--- a/solution.py
+++ b/solution.py
@@ -543,7 +543,7 @@
     def give(h, j):
         t_y[h].start_row(rem(y + 4 - j, 4), j == 0)
 
-    give(0, 0)
+    loop(0, 2, lambda j: give(0, j))
 
     t_pp.wait_recv()
     pos_exp = jnp.exp(logit_scale * jnp.sum(own_q[...].astype(F32) * v.pp[...].astype(F32), axis=1, keepdims=True))
@@ -565,7 +565,7 @@
     t_toth = Transfer(routes["home"], lambda i: v.tot, v.toth, s["toth"])
     t_totl.start()
     t_toth.start()
-    loop(1, 4, lambda j: give(0, j))
+    loop(2, 4, lambda j: give(0, j))
     loop(0, 4, lambda j: give(1, j))
 
     across = routes["xline"]

time: 98.5 us -> 99.3 us (level); the launches traced: 96.7 us -> 99 us
  Pallas kernels: 96 us -> 98.3 us
    pallas_call x1, Pallas kernels: 93.9 us -> 96.2 us  [shards(): pl.pallas_call(step_kernel, out_shape=[jax.ShapeDtypeStruct((n, EMB), BF1...]
where the time goes in v6:
time: 99.3 us; the launch traced here: 99 us
  Pallas kernels  98.3 us (99%)
    pallas_call x1, Pallas kernels, shards(): pl.pallas_call(step_kernel, out_shape=[jax.ShapeDtypeStruct((n, EMB), BF1...  96.2 us
    pallas_call x1, Pallas kernels, shards(): pl.pallas_call(settle_kernel, out_shape=[jax.ShapeDtypeStruct((n, EMB), B...  2.16 us

profile of v6, /device:TPU:24, one launch (start us, length us, event | category | flops | bytes accessed | tf_op | source)
XLA Modules:
  0.0 99.0 jit_solution(16991683519367322628)
XLA Ops:
  0.6 96.2 %contrastive_step.1 = (bf16[48,768]{1,0:T(8,128)(2,1)}, bf16[48,768]{1,0:T(8,128)(2,1)}, bf16[512,768]{1,0:T(8,128)(2,1)}) custom-call(bf16[2304,768]{1,0:T(8,128)(2,1)} %wq.1, bf16[3072,768]{1,0:T(8,128)(2,1)} %wp.1, bf16[192,2304]{1,0:T(8,128)(2,1)} %hq.1, bf16[48,3072]{1,0:T(8,128)(2,1)} %hp.1, bf16[512,3072]{1,0:T(8,128)(2,1)} %hpool.1, s32[8,192]{1,0:T(8,128)} %bitcast.1), custom_call_target="tpu_custom_call" | custom-call | tf_op jit(solution)/shard_map/contrastive_step/pallas_call | solution.py:685
  96.8 2.2 %settle.1 = (bf16[48,768]{1,0:T(8,128)(2,1)}, bf16[48,768]{1,0:T(8,128)(2,1)}, bf16[512,768]{1,0:T(8,128)(2,1)}) custom-call(bf16[48,768]{1,0:T(8,128)(2,1)} %get-tuple-element.6.q, bf16[48,768]{1,0:T(8,128)(2,1)} %get-tuple-element.7.p, bf16[512,768]{1,0:T(8,128)(2,1)} %get-tuple-element.8.n), custom_call_target="tpu_custom_call" | custom-call | tf_op jit(solution)/shard_map/settle/pallas_call | solution.py:696
